TPU v7x, 256 devices: a whole 4x4x8 slice. The times are simulated.
256 devices in a mesh: gx: 8 (over x, core), gy: 32 (over y, z).
Axes of the slice: x: 4, y: 4, z: 8, core: 2. Of those that a mesh axis runs over, the one named last changes fastest.
Arguments:
- features: float32 [64, 524288], P(None, ('gx', 'gy')), may hold values from -6 to 6
- cotangent: float32 [64, 524288], P(None, ('gx', 'gy')), may hold values from -6 to 6
- edge_src: int32 [8, 524288], P(None, ('gx', 'gy')), may hold values from 0 to 2559
- send_rows: int32 [4, 32768], P(None, ('gx', 'gy')), may hold values from 0 to 2047
- fine_to_coarse: int32 [524288], P(('gx', 'gy')), may hold values from 0 to 2047
- coarse_to_fine: int32 [524288], P(('gx', 'gy')), may hold values from 0 to 2047
- coarse_edges: int32 [2, 8192], replicated, may hold values from 0 to 2047
- edge_in: float32 [64, 128], replicated, may hold values from -0.5 to 0.5
- edge_out: float32 [64, 64], replicated, may hold values from -0.75 to 0.75
- node_in: float32 [64, 128], replicated, may hold values from -0.5 to 0.5
- node_out: float32 [64, 64], replicated, may hold values from -0.75 to 0.75
- coarse_in: float32 [64, 64], replicated, may hold values from -0.75 to 0.75
- coarse_out: float32 [64, 64], replicated, may hold values from -0.75 to 0.75
- coarse_mix: float32 [64, 64], replicated, may hold values from -0.75 to 0.75
- up_in: float32 [64, 128], replicated, may hold values from -0.5 to 0.5
- up_out: float32 [64, 64], replicated, may hold values from -0.75 to 0.75
- biases: float32 [4, 64], replicated, may hold values from -3 to 3
Outputs:
- output: float32 [64, 524288], P(None, ('gx', 'gy'))
- grad_features: float32 [64, 524288], P(None, ('gx', 'gy'))
- grad_edge_in: float32 [64, 128], replicated
- grad_edge_out: float32 [64, 64], replicated
- grad_node_in: float32 [64, 128], replicated
- grad_node_out: float32 [64, 64], replicated
- grad_coarse_in: float32 [64, 64], replicated
- grad_coarse_out: float32 [64, 64], replicated
- grad_coarse_mix: float32 [64, 64], replicated
- grad_up_in: float32 [64, 128], replicated
- grad_up_out: float32 [64, 64], replicated
- grad_biases: float32 [4, 64], replicated
Inputs may be any that keep to these rules, and one draw needn't show every extreme that they name: `edge_src`: indexes the receiver partition's 2048 own nodes, then the four received packets in the order of the first step. `send_rows`: partition-local node numbers.
All inputs are finite; a program needn't handle non-finite values.
Results may differ from a plain program's by a relative error of at most 0.0003.
Values sent between devices are 32-bit elements; how exact they have to be, the bound alone decides.
A program may use at most 64 MiB of HBM per device.

v0:
```python
from functools import partial
import math

import jax
import jax.numpy as jnp
from jax import lax
from jax.sharding import PartitionSpec as P

COARSE = 2048


def passed_along(value, axis, steps):
    count = lax.axis_size(axis)
    leading, last = (max(0, -steps), min(count, count - steps))
    return lax.ppermute(value, axis, [(source, source + steps) for source in range(leading, last)])


def matmul(left_side, right_side):
    return jnp.dot(
        left_side, right_side, precision=lax.Precision.HIGHEST, preferred_element_type=jnp.float32
    )


def swish(values):
    return values * jax.nn.sigmoid(values)


def fine_update(
    latent, extended, edge_in, edge_out, node_in, node_out, edge_bias, node_bias, sources
):
    feature_count = latent.shape[0]
    receiver_part = matmul(edge_in[:, :feature_count], latent)
    sender_part = matmul(edge_in[:, feature_count:], extended)
    hidden = swish(receiver_part[:, None, :] + sender_part[:, sources] + edge_bias[:, None, None])
    summed = matmul(edge_out, jnp.sum(hidden, axis=1))
    activation = swish(
        matmul(node_in[:, :feature_count], latent)
        + matmul(node_in[:, feature_count:], summed)
        + node_bias[:, None]
    )
    return latent + matmul(node_out, activation)


def coarse_node(pooled, coarse_in, coarse_out, coarse_bias):
    return pooled + matmul(coarse_out, swish(matmul(coarse_in, pooled) + coarse_bias[:, None]))


def coarse_edge(nodes, coarse_mix, coarse_edges):
    gathered = nodes[:, coarse_edges[0]]
    summed = jnp.zeros_like(nodes).at[:, coarse_edges[1]].add(gathered)
    factor = (nodes.shape[1] / coarse_edges.shape[1]) ** 0.5
    return nodes + matmul(coarse_mix, summed) * factor


def up_update(middle, looked, up_in, up_out, up_bias):
    feature_count = middle.shape[0]
    activation = swish(
        matmul(up_in[:, :feature_count], middle)
        + matmul(up_in[:, feature_count:], looked)
        + up_bias[:, None]
    )
    return middle + matmul(up_out, activation)


def block_width(node_count):
    return math.gcd(node_count, 1024)


def one_hot_block(index_block, table_width):
    return (index_block[:, None] == jnp.arange(table_width, dtype=jnp.int32)[None, :]).astype(
        jnp.float32
    )


def pool_nodes(values, index, table_width):
    feature_count, node_count = values.shape
    width = block_width(node_count)
    blocks = node_count // width
    value_blocks = values.reshape(feature_count, blocks, width).transpose(1, 0, 2)
    index_blocks = index.reshape(blocks, width)

    def add_block(total, items):
        return (total + matmul(items[0], one_hot_block(items[1], table_width)), None)

    start = jnp.zeros((feature_count, table_width), jnp.float32)
    total, unused = lax.scan(add_block, start, (value_blocks, index_blocks))
    return total


def look_nodes(table, index):
    feature_count, table_width = table.shape
    node_count = index.shape[0]
    width = block_width(node_count)
    blocks = node_count // width
    index_blocks = index.reshape(blocks, width)

    def read_block(index_block):
        selector = one_hot_block(index_block, table_width)
        return lax.dot_general(
            table,
            selector,
            (((1,), (1,)), ((), ())),
            precision=lax.Precision.HIGHEST,
            preferred_element_type=jnp.float32,
        )

    result = lax.map(read_block, index_blocks)
    return result.transpose(1, 0, 2).reshape(feature_count, node_count)


def pass_rows(packet, offset):
    return passed_along(packet, "gx", offset)


def pass_cols(packet, offset):
    return passed_along(packet, "gy", offset)


def coarse_total(table):
    return lax.psum(table, ("gx", "gy"))


def local(
    features,
    cotangent,
    edge_src,
    send_rows,
    fine_to_coarse,
    coarse_to_fine,
    coarse_edges,
    edge_in,
    edge_out,
    node_in,
    node_out,
    coarse_in,
    coarse_out,
    coarse_mix,
    up_in,
    up_out,
    biases,
):
    local_nodes = features.shape[1]
    halo_rows = send_rows.shape[1]
    pool_scale = (COARSE / (local_nodes * lax.axis_size("gx") * lax.axis_size("gy"))) ** 0.5
    packets = features[:, send_rows]
    extended = jnp.concatenate(
        [
            features,
            pass_rows(packets[:, 0], 1),
            pass_rows(packets[:, 1], -1),
            pass_cols(packets[:, 2], 1),
            pass_cols(packets[:, 3], -1),
        ],
        axis=1,
    )
    middle, fine_back = jax.vjp(
        partial(fine_update, sources=edge_src),
        features,
        extended,
        edge_in,
        edge_out,
        node_in,
        node_out,
        biases[0],
        biases[1],
    )
    pooled_part = pool_nodes(middle, fine_to_coarse, COARSE) * pool_scale
    pooled = coarse_total(pooled_part)
    nodes, node_back = jax.vjp(coarse_node, pooled, coarse_in, coarse_out, biases[2])
    mixed, mix_back = jax.vjp(partial(coarse_edge, coarse_edges=coarse_edges), nodes, coarse_mix)
    looked = look_nodes(mixed, coarse_to_fine)
    output, up_back = jax.vjp(up_update, middle, looked, up_in, up_out, biases[3])
    grad_middle, grad_looked, grad_up_in, grad_up_out, grad_up_bias = up_back(cotangent)
    grad_mixed_part = pool_nodes(grad_looked, coarse_to_fine, COARSE)
    grad_nodes_part, grad_mix = mix_back(grad_mixed_part)
    grad_nodes = coarse_total(grad_nodes_part)
    grad_pooled, grad_coarse_in, grad_coarse_out, grad_coarse_bias = node_back(grad_nodes)
    grad_middle = grad_middle + look_nodes(grad_pooled, fine_to_coarse) * pool_scale
    (
        grad_own,
        grad_ext,
        grad_edge_in,
        grad_edge_out,
        grad_node_in,
        grad_node_out,
        grad_edge_bias,
        grad_node_bias,
    ) = fine_back(grad_middle)
    pieces = [
        grad_ext[:, local_nodes + slot * halo_rows : local_nodes + (slot + 1) * halo_rows]
        for slot in range(4)
    ]
    returned = jnp.stack(
        [
            pass_rows(pieces[0], -1),
            pass_rows(pieces[1], 1),
            pass_cols(pieces[2], -1),
            pass_cols(pieces[3], 1),
        ],
        axis=1,
    )
    grad_features = (
        grad_own
        + grad_ext[:, :local_nodes]
        + jnp.zeros_like(features).at[:, send_rows].add(returned)
    )
    fine_biases = jnp.stack([grad_edge_bias, grad_node_bias, grad_up_bias])
    summed = lax.psum(
        (
            grad_edge_in,
            grad_edge_out,
            grad_node_in,
            grad_node_out,
            grad_mix,
            grad_up_in,
            grad_up_out,
            fine_biases,
        ),
        ("gx", "gy"),
    )
    grad_biases = jnp.stack([summed[7][0], summed[7][1], grad_coarse_bias, summed[7][2]])
    return (
        output,
        grad_features,
        summed[0],
        summed[1],
        summed[2],
        summed[3],
        grad_coarse_in,
        grad_coarse_out,
        summed[4],
        summed[5],
        summed[6],
        grad_biases,
    )


def solution(mesh):
    in_specs = (
        P(None, ("gx", "gy")),
        P(None, ("gx", "gy")),
        P(None, ("gx", "gy")),
        P(None, ("gx", "gy")),
        P(("gx", "gy")),
        P(("gx", "gy")),
        P(),
        P(),
        P(),
        P(),
        P(),
        P(),
        P(),
        P(),
        P(),
        P(),
        P(),
    )
    out_specs = (
        P(None, ("gx", "gy")),
        P(None, ("gx", "gy")),
        P(),
        P(),
        P(),
        P(),
        P(),
        P(),
        P(),
        P(),
        P(),
        P(),
    )
    return jax.shard_map(local, mesh=mesh, in_specs=in_specs, out_specs=out_specs, check_vma=False)
```

profile of v0, /device:TPU:1, one launch (start us, length us, event | category | flops | bytes accessed | tf_op | source)
XLA Modules:
  0.0 1284.1 jit_solution(6008554091809120378)
XLA Ops:
  11.8 5.0 collective-permute-start.2
  16.8 4.7 collective-permute-start.1
  21.5 1.9 collective-permute-start
  27.1 2.9 fusion.81
  30.0 2.9 fusion.102
  38.6 54.7 %gather_fusion.1 = f32[16384,64]{1,0:T(8,128)} fusion(f32[64,2560]{0,1:T(8,128)S(1)} %copy.65, s32[16384]{0:T(1024)S(1)} %broadcast_clamp_fusion), kind=kCustom, calls=%fused_computation.1 | custom fusion | bytes 8454144 | tf_op jit(solution)/shard_map/jvp()/gather | solution.py:34
  93.4 4.8 multiply_reduce_fusion
  103.2 7.0 while.44
  103.2 3.5 fusion.178
  106.7 3.5 fusion.178
  112.9 251.2 %all-reduce.11.cloned.1.call-done = f32[64,2048]{1,0:T(8,128)} async-done(((f32[64,2048]{1,0:T(8,128)}), f32[64,2048]{1,0:T(8,128)}) %all-reduce.11.cloned.1.call-update) | async-done | bytes 524304 | tf_op jit(solution)/shard_map/psum | solution.py:120
  369.7 90.4 %scatter_custom_fusion = f32[64,2048]{0,1:T(8,128)S(1)} fusion(s32[8192]{0:T(1024)} %bitcast.245, f32[64,2048]{0,1:T(8,128)} %copy.67, s32[8192]{0:T(1024)} %broadcast_clamp_fusion.2, f32[]{:T(128)} %constant.19.clone.1), kind=kCustom, calls=%fused_computation.44 | custom fusion | flops 524288 | bytes 524800 | tf_op jit(solution)/shard_map/jvp()/scatter-add | solution.py:50
  460.1 2.1 fusion.29
  462.3 11.0 while.42
  462.3 5.5 fusion.174
  467.8 5.5 fusion.174
  473.3 2.2 fusion.96
  475.5 2.3 convolution_bitcast_fusion.14
  477.8 2.6 fusion.37
  484.3 10.4 while.45
  484.3 5.1 fusion.180
  489.4 5.3 fusion.180
  494.6 2.5 convolution_bitcast_fusion.7
  497.1 2.4 copy.71
  499.5 2.4 copy.70
  501.8 103.6 %scatter_custom_fusion.1 = f32[64,2048]{0,1:T(8,128)} fusion(f32[64,2048]{0,1:T(8,128)} %copy.71, s32[8192]{0:T(1024)} %bitcast.243, f32[]{:T(128)} %constant.19.clone.1, pred[8192]{0:T(1024)(128)(4,1)S(1)} %compare_and_fusion, f32[64,2048]{0,1:T(8,128)} %copy.70, s32[8192]{0:T(1024)S(1)} %broadcast_clamp_fusion.1), kind=kCustom, calls=%fused_computation.42 | custom fusion | flops 1048576 | bytes 1614336 | tf_op jit(solution)/shard_map/transpose(jvp())/scatter-add | solution.py:49
  605.4 2.3 copy.72
  607.8 2.4 fusion.55
  610.2 248.5 %all-reduce.13.cloned.1.call-done = f32[64,2048]{1,0:T(8,128)} async-done(((f32[64,2048]{1,0:T(8,128)}), f32[64,2048]{1,0:T(8,128)}) %all-reduce.13.cloned.1.call-update) | async-done | bytes 524304 | tf_op jit(solution)/shard_map/psum | solution.py:120
  858.7 2.6 fusion.100
  863.9 8.9 while.43
  863.9 4.4 fusion.176
  868.4 4.4 fusion.176
  876.5 2.6 fusion.62
  879.1 1.9 fusion.99
  888.2 5.7 fusion.21
  894.0 3.2 copy-done.1
  897.2 2.5 fusion.95
  899.7 2.5 fusion.104
  902.1 2.1 convolution_bitcast_fusion.13
  904.2 88.0 %scatter_custom_fusion.2 = f32[64,2560]{0,1:T(8,128)S(1)} fusion(s32[16384]{0:T(1024)S(1)} %bitcast.240, f32[16384,64]{1,0:T(8,128)} %bitcast.227, f32[]{:T(128)} %constant.19.clone.1), kind=kCustom, calls=%fused_computation.85 | custom fusion | flops 1048576 | bytes 655872 | tf_op jit(solution)/shard_map/transpose(jvp())/scatter-add | solution.py:34
  992.2 2.2 fusion.103
  997.9 3.9 collective-permute-start.4
  1004.5 4.0 collective-permute-start.5
  1012.1 2.5 fusion.65
  1014.6 2.4 fusion.108
  1017.5 3.7 scatter_fusion
  1022.4 243.2 %all-reduce.15.cloned.1.call-done = (f32[64,128]{1,0:T(8,128)}, f32[64,64]{1,0:T(8,128)}, f32[64,128]{1,0:T(8,128)}, f32[64,64]{1,0:T(8,128)}, f32[64,64]{1,0:T(...) async-done(((f32[64,128]{1,0:T(8,128)}, f32[64,64]{1,0:T(8,128)}, f32[64,128]{1,0:T(8,128)}, f32[64,64]{1,0:T(8,128)}, f32[64,64]{1,0:T(8,128)}, ...) | async-done | bytes 164624 | tf_op jit(solution)/shard_map/psum | solution.py:208
  (159 shorter events, 67.3 us)
Async XLA Ops:
  7.2 359.4 %copy-start = (f32[64,64]{1,0:T(8,128)S(1)}, f32[64,64]{1,0:T(8,128)}, u32[]{:S(2)}) copy-start(f32[64,64]{1,0:T(8,128)} %param.37) | copy-start | bytes 49156
  7.2 356.9 %all-reduce.11.cloned.1.call-start = ((), (), s32[]{:S(2)}) async-start(), calls=%async_computation | async-start | bytes 1048576 | tf_op jit(solution)/shard_map/psum | solution.py:120
  10.5 25.3 %collective-permute-start.3 = (f32[64,128]{1,0:T(8,128)S(1)}, f32[64,128]{1,0:T(8,128)S(1)}, u32[]{:S(2)}, u32[]{:S(2)}) collective-permute-start(f32[64,128]{1,0:T(8,128)S(1)} %get-tuple-element.218), channel_id=1, source_target_pairs={{1,0},{2,1},{3,2},{4,3},{5,4},{6,5},{7,6},{8,7},{9,8},{10,9},{11,1... | collective-permute-start | bytes 98312 | tf_op jit(solution)/shard_map/ppermute | solution.py:15
  11.8 24.0 %collective-permute-start.2 = (f32[64,128]{1,0:T(8,128)S(1)}, f32[64,128]{1,0:T(8,128)S(1)}, u32[]{:S(2)}, u32[]{:S(2)}) collective-permute-start(f32[64,128]{1,0:T(8,128)S(1)} %get-tuple-element.219), channel_id=1, source_target_pairs={{0,1},{1,2},{2,3},{3,4},{4,5},{5,6},{6,7},{7,8},{8,9},{9,10},{10,1... | collective-permute-start | bytes 98312 | tf_op jit(solution)/shard_map/ppermute | solution.py:15
  16.8 19.0 %collective-permute-start.1 = (f32[64,128]{1,0:T(8,128)S(1)}, f32[64,128]{1,0:T(8,128)S(1)}, u32[]{:S(2)}, u32[]{:S(2)}) collective-permute-start(f32[64,128]{1,0:T(8,128)S(1)} %get-tuple-element.220), channel_id=1, source_target_pairs={{32,0},{64,32},{96,64},{128,96},{160,128},{192,160},{224,192},{33,... | collective-permute-start | bytes 98312 | tf_op jit(solution)/shard_map/ppermute | solution.py:15
  21.5 14.3 %collective-permute-start = (f32[64,128]{1,0:T(8,128)S(1)}, f32[64,128]{1,0:T(8,128)S(1)}, u32[]{:S(2)}, u32[]{:S(2)}) collective-permute-start(f32[64,128]{1,0:T(8,128)S(1)} %get-tuple-element.221), channel_id=1, source_target_pairs={{0,32},{32,64},{64,96},{96,128},{128,160},{160,192},{192,224},{1,3... | collective-permute-start | bytes 98312 | tf_op jit(solution)/shard_map/ppermute | solution.py:15
  26.4 6.4 copy-start.24
  26.4 12.2 copy-start.23
  30.0 63.4 %copy-start.3 = (f32[64,2048]{0,1:T(8,128)}, f32[64,2048]{0,1:T(8,128)S(1)}, u32[]{:S(2)}) copy-start(f32[64,2048]{0,1:T(8,128)S(1)} %fusion.81) | copy-start | bytes 1572868
  35.8 0.9 copy-start.5
  93.3 4.9 copy-start.22
  93.3 7.0 copy-start.18
  93.3 7.6 copy-start.2
  93.3 9.0 copy-start.29
  93.4 9.8 copy-start.16
  99.5 0.8 copy-start.7
  101.5 0.8 copy-start.15
  103.1 8.3 copy-start.9
  103.2 8.2 copy-start.26
  103.2 8.3 copy-start.19
  103.2 260.9 %copy-start.21 = (f32[64,64]{1,0:T(8,128)S(1)}, f32[64,64]{1,0:T(8,128)}, u32[]{:S(2)}) copy-start(f32[64,64]{1,0:T(8,128)} %param.36) | copy-start | bytes 49156
  110.2 349.9 %copy-start.20 = (f32[64,64]{1,0:T(8,128)S(1)}, f32[64,64]{1,0:T(8,128)}, u32[]{:S(2)}) copy-start(f32[64,64]{1,0:T(8,128)} %param.38) | copy-start | bytes 49156
  111.1 747.7 %all-reduce.13.cloned.1.call-start = ((), (), s32[]{:S(2)}) async-start(), calls=%async_computation.1 | async-start | bytes 1048576 | tf_op jit(solution)/shard_map/psum | solution.py:120
  365.7 0.8 copy-start.17
  462.3 11.1 copy-start.28
  462.3 15.5 %copy-start.25 = (f32[64,64]{1,0:T(8,128)S(1)}, f32[64,64]{1,0:T(8,128)}, u32[]{:S(2)}) copy-start(f32[64,64]{1,0:T(8,128)} %param.40) | copy-start | bytes 49156
  473.3 8.3 copy-start.10
  607.8 657.8 %all-reduce.15.cloned.1.call-start = ((), (), s32[]{:S(2)}) async-start(), calls=%async_computation.2 | async-start | bytes 462848 | tf_op jit(solution)/shard_map/psum | solution.py:208
  861.3 0.8 copy-start.11
  863.9 15.3 %copy-start.30 = (f32[64,64]{1,0:T(8,128)S(1)}, f32[64,64]{1,0:T(8,128)}, u32[]{:S(2)}) copy-start(f32[64,64]{1,0:T(8,128)} %param.35) | copy-start | bytes 49156
  872.8 0.8 copy-start.12
  873.6 7.4 copy-start.8
  873.6 14.6 %copy-start.4 = (f32[64,2048]{0,1:T(8,128)S(1)}, f32[64,2048]{0,1:T(8,128)}, u32[]{:S(2)}) copy-start(f32[64,2048]{0,1:T(8,128)} %copy-done.3) | copy-start | bytes 1572868
  876.5 5.7 copy-start.13
  894.0 3.2 copy-start.1
  897.2 4.9 copy-start.14
  897.2 95.0 %copy-start.6 = (f32[64,2560]{1,0:T(8,128)S(1)}, f32[64,2560]{1,0:T(8,128)}, u32[]{:S(2)}) copy-start(f32[64,2560]{1,0:T(8,128)} %copy-done.5) | copy-start | bytes 1966084
  992.2 276.1 %copy-start.27 = (f32[64]{0:T(128)S(1)}, f32[64]{0:T(128)}, u32[]{:S(2)}) copy-start(f32[64]{0:T(128)} %get-tuple-element.231) | copy-start | bytes 772
  997.9 19.4 %collective-permute-start.4 = (f32[64,128]{1,0:T(8,128)S(1)}, f32[64,128]{1,0:T(8,128)S(1)}, u32[]{:S(2)}, u32[]{:S(2)}) collective-permute-start(f32[64,128]{1,0:T(8,128)S(1)} %get-tuple-element.214), channel_id=1, source_target_pairs={{32,0},{64,32},{96,64},{128,96},{160,128},{192,160},{224,192},{33,... | collective-permute-start | bytes 98312 | tf_op jit(solution)/shard_map/ppermute | solution.py:15
  1001.9 15.5 %collective-permute-start.7 = (f32[64,128]{1,0:T(8,128)S(1)}, f32[64,128]{1,0:T(8,128)S(1)}, u32[]{:S(2)}, u32[]{:S(2)}) collective-permute-start(f32[64,128]{1,0:T(8,128)S(1)} %get-tuple-element.215), channel_id=1, source_target_pairs={{0,1},{1,2},{2,3},{3,4},{4,5},{5,6},{6,7},{7,8},{8,9},{9,10},{10,1... | collective-permute-start | bytes 98312 | tf_op jit(solution)/shard_map/ppermute | solution.py:15
  1003.2 14.2 %collective-permute-start.6 = (f32[64,128]{1,0:T(8,128)S(1)}, f32[64,128]{1,0:T(8,128)S(1)}, u32[]{:S(2)}, u32[]{:S(2)}) collective-permute-start(f32[64,128]{1,0:T(8,128)S(1)} %get-tuple-element.216), channel_id=1, source_target_pairs={{1,0},{2,1},{3,2},{4,3},{5,4},{6,5},{7,6},{8,7},{9,8},{10,9},{11,1... | collective-permute-start | bytes 98312 | tf_op jit(solution)/shard_map/ppermute | solution.py:15
  1004.5 12.9 %collective-permute-start.5 = (f32[64,128]{1,0:T(8,128)S(1)}, f32[64,128]{1,0:T(8,128)S(1)}, u32[]{:S(2)}, u32[]{:S(2)}) collective-permute-start(f32[64,128]{1,0:T(8,128)S(1)} %get-tuple-element.217), channel_id=1, source_target_pairs={{0,32},{32,64},{64,96},{96,128},{128,160},{160,192},{192,224},{1,3... | collective-permute-start | bytes 98312 | tf_op jit(solution)/shard_map/ppermute | solution.py:15
Sparse Core Ops, SparseCore 0:
  111.2 252.8 all-reduce.10
  607.9 250.7 all-reduce.12
  1012.2 253.2 all-reduce.14
where the time goes:
time: 1300 us; the launch traced here: 1280 us
  waiting for transfers between devices  743 us (57%)
  other arithmetic  308 us (24%)
  matrix products  101 us (8%)
  local copies, waits for them, and re-layouts  93.4 us (7%)
  starting transfers between devices  23.8 us (2%)
  between operations  15 us (1%)
    psum x2, waiting for transfers between devices, coarse_total(): return lax.psum(table, ('gx', 'gy'))  500 us
    psum x1, waiting for transfers between devices, local(): lax.psum((grad_edge_in, grad_edge_out, grad_node_in, grad_node_out, grad_...  243 us
    scatter-add x1, other arithmetic, coarse_edge(): gathered = nodes[:, coarse_edges[0]]  104 us
    scatter-add x1, other arithmetic, coarse_edge(): summed = jnp.zeros_like(nodes).at[:, coarse_edges[1]].add(gathered)  90.4 us
    scatter-add x1, other arithmetic, fine_update(): sender_part[:, sources]  88 us
    dot_general x40, matrix products, matmul(): jnp.dot(left_side, right_side, precision=lax.Precision.HIGHEST, preferred...  80.9 us
    gather x1, local copies, waits for them, and re-layouts, fine_update(): sender_part[:, sources]  54.7 us
  transfers between devices with their start and end apart: 11, of which 3 were waited for; matrix products, arithmetic and copies ran while one was open for 2% of the time, Pallas kernels for 0%

commit v1 on v0

--- a/solution.py
+++ b/solution.py
@@ -4,9 +4,117 @@
 import jax
 import jax.numpy as jnp
 from jax import lax
+from jax.experimental import pallas as pl
+from jax.experimental.pallas import tpu as pltpu
 from jax.sharding import PartitionSpec as P
 
 COARSE = 2048
+MESH = pl.DeviceIdType.MESH
+
+
+def add_up_kernel(tiles, x_ref, o_ref, parts, row_sum, tile_parts, tile_sum, full,
+                  send1, recv1, send2, recv2, send3, recv3, send4, recv4):
+    gx, gy = lax.axis_index("gx"), lax.axis_index("gy")
+    barrier = pltpu.get_barrier_semaphore()
+
+    def greet_row(k, carry):
+        pl.semaphore_signal(barrier, inc=1, device_id=(lax.rem(gx + k, 8), gy), device_id_type=MESH)
+        return carry
+
+    def greet_col(k, carry):
+        pl.semaphore_signal(barrier, inc=1, device_id=(gx, lax.rem(gy + k, 32)), device_id_type=MESH)
+        return carry
+
+    lax.fori_loop(1, 8, greet_row, 0)
+    lax.fori_loop(1, 32, greet_col, 0)
+    pl.semaphore_wait(barrier, 38)
+
+    def scatter_row(k):
+        peer = lax.rem(gx + k, 8)
+        return pltpu.make_async_remote_copy(
+            src_ref=x_ref.at[pl.ds(pl.multiple_of(peer * 8, 8), 8)], dst_ref=parts.at[k],
+            send_sem=send1.at[k], recv_sem=recv1.at[k],
+            device_id=(peer, gy), device_id_type=MESH)
+
+    def scatter_col(k):
+        peer = lax.rem(gy + k, 32)
+        return pltpu.make_async_remote_copy(
+            src_ref=row_sum.at[lax.rem(peer, tiles)], dst_ref=tile_parts.at[gy],
+            send_sem=send2.at[k], recv_sem=recv2.at[k],
+            device_id=(gx, peer), device_id_type=MESH)
+
+    mine = lax.rem(gy, tiles)
+    block = gy - mine
+
+    def gather_col(k):
+        peer = block + lax.rem(mine + k, tiles)
+        return pltpu.make_async_remote_copy(
+            src_ref=tile_sum.at[mine], dst_ref=tile_sum.at[mine],
+            send_sem=send3.at[k], recv_sem=recv3.at[k],
+            device_id=(gx, peer), device_id_type=MESH)
+
+    rows = pl.ds(pl.multiple_of(gx * 8, 8), 8)
+
+    def gather_row(k):
+        return pltpu.make_async_remote_copy(
+            src_ref=full.at[rows], dst_ref=full.at[rows],
+            send_sem=send4.at[k], recv_sem=recv4.at[k],
+            device_id=(lax.rem(gx + k, 8), gy), device_id_type=MESH)
+
+    def start_all(make, count):
+        def body(k, carry):
+            make(k).start()
+            return carry
+        lax.fori_loop(1, count, body, 0)
+
+    def wait_all(make, count):
+        def body(k, carry):
+            make(k).wait()
+            return carry
+        lax.fori_loop(1, count, body, 0)
+
+    start_all(scatter_row, 8)
+    wait_all(scatter_row, 8)
+    total = x_ref[rows]
+    for k in range(1, 8):
+        total = total + parts[k]
+    for tile in range(tiles):
+        row_sum[tile] = total[:, tile * 128:(tile + 1) * 128]
+    start_all(scatter_col, 32)
+    tile_parts[gy] = row_sum[mine]
+    wait_all(scatter_col, 32)
+    tile_total = tile_parts[0]
+    for k in range(1, 32):
+        tile_total = tile_total + tile_parts[k]
+    tile_sum[mine] = tile_total
+    start_all(gather_col, tiles)
+    wait_all(gather_col, tiles)
+    for tile in range(tiles):
+        full[rows, tile * 128:(tile + 1) * 128] = tile_sum[tile]
+    start_all(gather_row, 8)
+    wait_all(gather_row, 8)
+    o_ref[...] = full[...]
+
+
+def add_up(table, collective_id):
+    width = table.shape[1]
+    tiles = width // 128
+    dma = pltpu.SemaphoreType.DMA
+    return pl.pallas_call(
+        partial(add_up_kernel, tiles),
+        out_shape=jax.ShapeDtypeStruct(table.shape, jnp.float32),
+        in_specs=[pl.BlockSpec(memory_space=pltpu.VMEM)],
+        out_specs=pl.BlockSpec(memory_space=pltpu.VMEM),
+        scratch_shapes=[
+            pltpu.VMEM((8, 8, width), jnp.float32),
+            pltpu.VMEM((tiles, 8, 128), jnp.float32),
+            pltpu.VMEM((32, 8, 128), jnp.float32),
+            pltpu.VMEM((tiles, 8, 128), jnp.float32),
+            pltpu.VMEM((64, width), jnp.float32),
+            dma((8,)), dma((8,)), dma((32,)), dma((32,)), dma((tiles,)), dma((tiles,)), dma((8,)), dma((8,)),
+        ],
+        compiler_params=pltpu.CompilerParams(collective_id=collective_id, has_side_effects=True),
+    )(table)
 
 
 def passed_along(value, axis, steps):
@@ -117,7 +225,7 @@
 
 
 def coarse_total(table):
-    return lax.psum(table, ("gx", "gy"))
+    return add_up(table, 0)
 
 
 def local(
@@ -205,19 +313,18 @@
         + jnp.zeros_like(features).at[:, send_rows].add(returned)
     )
     fine_biases = jnp.stack([grad_edge_bias, grad_node_bias, grad_up_bias])
-    summed = lax.psum(
-        (
-            grad_edge_in,
-            grad_edge_out,
-            grad_node_in,
-            grad_node_out,
-            grad_mix,
-            grad_up_in,
-            grad_up_out,
-            fine_biases,
-        ),
-        ("gx", "gy"),
-    )
+    flat = jnp.concatenate([
+        part.reshape(-1)
+        for part in (grad_edge_in, grad_edge_out, grad_node_in, grad_node_out, grad_mix,
+                     grad_up_in, grad_up_out, fine_biases)])
+    count = flat.shape[0]
+    whole = add_up(jnp.pad(flat, (0, 64 * 1024 - count)).reshape(64, 1024), 1).reshape(-1)
+    shapes = ((64, 128), (64, 64), (64, 128), (64, 64), (64, 64), (64, 128), (64, 64), (3, 64))
+    summed, offset = [], 0
+    for shape in shapes:
+        size = shape[0] * shape[1]
+        summed.append(whole[offset:offset + size].reshape(shape))
+        offset += size
     grad_biases = jnp.stack([summed[7][0], summed[7][1], grad_coarse_bias, summed[7][2]])
     return (
         output,

time: 1300 us -> 621 us (0.48)
  waiting for transfers between devices: 743 us -> 0.02 us
  Pallas kernels: 0 us -> 104 us
  other arithmetic: 308 us -> 294 us
  between operations: 15 us -> 1.98 us
    psum x3 -> x0, waiting for transfers between devices: 743 us -> none  [the longest x2 500 us: coarse_total(): return lax.psum(table, ('gx', 'gy'))]
    pallas_call x0 -> x3, Pallas kernels: none -> 104 us  [add_up(): pl.pallas_call(partial(add_up_kernel, tiles), out_shape=jax.ShapeDtypeStr...]
  transfers between devices with their start and end apart: 11 -> 8, of which waited for: 3 -> 0; matrix products, arithmetic and copies ran while one was open for 2% -> 3% of each run, Pallas kernels for 0% -> 0%
where the time goes in v1:
time: 621 us; the launch traced here: 612 us
  other arithmetic  294 us (47%)
  Pallas kernels  104 us (17%)
  matrix products  98.1 us (16%)
  local copies, waits for them, and re-layouts  90.1 us (15%)
  starting transfers between devices  23.2 us (4%)
    pallas_call x3, Pallas kernels, add_up(): pl.pallas_call(partial(add_up_kernel, tiles), out_shape=jax.ShapeDtypeStr...  104 us
    scatter-add x1, other arithmetic, coarse_edge(): gathered = nodes[:, coarse_edges[0]]  92.4 us
    scatter-add x1, other arithmetic, coarse_edge(): summed = jnp.zeros_like(nodes).at[:, coarse_edges[1]].add(gathered)  90.8 us
    scatter-add x1, other arithmetic, fine_update(): sender_part[:, sources]  88.2 us
    dot_general x40, matrix products, matmul(): jnp.dot(left_side, right_side, precision=lax.Precision.HIGHEST, preferred...  78.3 us
    gather x1, local copies, waits for them, and re-layouts, fine_update(): sender_part[:, sources]  54.6 us
    ppermute x8, starting transfers between devices, passed_along(): lax.ppermute(value, axis, [(source, source + steps) for source in range(l...  23.2 us
    dot_general x4, matrix products, read_block(): lax.dot_general(table, selector, (((1,), (1,)), ((), ())), precision=lax....  19.8 us
  transfers between devices with their start and end apart: 8, of which 0 were waited for; matrix products, arithmetic and copies ran while one was open for 3% of the time, Pallas kernels for 0%

profile of v1, /device:TPU:1, one launch (start us, length us, event | category | flops | bytes accessed | tf_op | source)
XLA Modules:
  0.0 612.1 jit_solution(7329307184860178658)
XLA Ops:
  5.2 5.0 collective-permute-start.2
  10.2 4.7 collective-permute-start.1
  14.9 1.9 collective-permute-start
  21.4 2.9 fusion.81
  24.3 2.9 fusion.104
  32.2 54.6 %gather_fusion.1 = f32[16384,64]{1,0:T(8,128)} fusion(f32[64,2560]{0,1:T(8,128)S(1)} %copy.64, s32[16384]{0:T(1024)S(1)} %broadcast_clamp_fusion), kind=kCustom, calls=%fused_computation.1 | custom fusion | bytes 8454144 | tf_op jit(solution)/shard_map/jvp()/gather | solution.py:142
  86.8 4.8 multiply_reduce_fusion
  96.7 7.0 %while.44 = (s32[]{:T(128)}, f32[64,2048]{1,0:T(8,128)S(1)}, f32[2,64,1024]{2,1,0:T(8,128)S(1)}, s32[2,1024]{1,0:T(2,128)S(1)}, s32[]{:T(128)}, /*index=5*/s32[]{:T(128)}) while((s32[]{:T(128)}, f32[64,2048]{1,0:T(8,128)S(1)}, f32[2,64,1024]{2,1,0:T(8,128)S(1)}, s32[2,1024]{1,0:T(2,128)S(1)}, s32[]{:T(128)}, ...), condition=%wide.region_2.3_spmd.clone, body=%wide.region_1.2_spmd.clone.sunk | while | flops 1612972032 | bytes 1323103 | solution.py:194
  96.8 3.5 fusion.180
  100.2 3.5 fusion.180
  104.6 40.0 %shard_map.256 = f32[64,2048]{1,0:T(8,128)} custom-call(f32[64,2048]{1,0:T(8,128)} %broadcast_multiply_fusion.x_ref), custom_call_target="tpu_custom_call" | custom-call | tf_op jit(solution)/shard_map/pallas_call | solution.py:103
  148.4 1.8 fusion.38
  151.5 90.8 %scatter_custom_fusion = f32[64,2048]{0,1:T(8,128)S(1)} fusion(s32[8192]{0:T(1024)S(1)} %bitcast.261, f32[64,2048]{0,1:T(8,128)} %copy.66, s32[8192]{0:T(1024)} %broadcast_clamp_fusion.2, f32[]{:T(128)} %constant.20.clone.1), kind=kCustom, calls=%fused_computation.44 | custom fusion | flops 524288 | bytes 524800 | tf_op jit(solution)/shard_map/jvp()/scatter-add | solution.py:158
  242.4 2.1 fusion.29
  244.6 11.0 %while.42 = (s32[]{:T(128)}, f32[2,64,1024]{2,1,0:T(8,128)S(1)}, s32[2,1024]{1,0:T(2,128)S(1)}, f32[64,2048]{1,0:T(8,128)}, s32[]{:T(128)}) while((s32[]{:T(128)}, f32[2,64,1024]{2,1,0:T(8,128)S(1)}, s32[2,1024]{1,0:T(2,128)S(1)}, f32[64,2048]{1,0:T(8,128)}, s32[]{:T(128)}) %tuple.97), condition=%wide.region_5.6_spmd, body=%wide.region_4.5_spmd.sunk | while | flops 1612709888 | bytes 798797 | solution.py:215
  244.6 5.5 fusion.176
  250.1 5.5 fusion.176
  255.6 2.2 fusion.96
  257.8 2.3 convolution_bitcast_fusion.14
  260.1 2.6 fusion.37
  266.6 10.3 %while.45 = (s32[]{:T(128)}, f32[64,2048]{1,0:T(8,128)}, f32[2,64,1024]{2,1,0:T(8,128)}, s32[2,1024]{1,0:T(2,128)S(1)}, s32[]{:T(128)}, /*index=5*/s32[]{:T(128)}) while((s32[]{:T(128)}, f32[64,2048]{1,0:T(8,128)}, f32[2,64,1024]{2,1,0:T(8,128)}, s32[2,1024]{1,0:T(2,128)S(1)}, s32[]{:T(128)}, /*index=5*/s32[]{:T(128)}) %tuple.110), condition=%wide.region_7.8_spmd.clone, body=%wide.region_6.7_spmd.clone.sunk | while | flops 1612972032 | bytes 1323103 | solution.py:194
  266.6 5.1 fusion.182
  271.6 5.2 fusion.182
  276.9 2.4 fusion.55
  281.0 2.4 copy.70
  284.7 92.4 %scatter_custom_fusion.1 = f32[64,2048]{0,1:T(8,128)} fusion(f32[64,2048]{0,1:T(8,128)} %copy.70, s32[8192]{0:T(1024)S(1)} %bitcast.259, f32[]{:T(128)} %constant.20.clone.1, pred[8192]{0:T(1024)(128)(4,1)S(1)} %compare_and_fusion, f32[64,2048]{0,1:T(8,128)} %copy.69, s32[8192]{0:T(1024)S(1)} %broadcast_clamp_fusion.1), kind=kCustom, calls=%fused_computation.42 | custom fusion | flops 1048576 | bytes 1614336 | tf_op jit(solution)/shard_map/transpose(jvp())/scatter-add | solution.py:157
  377.1 2.3 copy.71.x_ref
  379.5 35.0 %shard_map.257 = f32[64,2048]{1,0:T(8,128)} custom-call(f32[64,2048]{1,0:T(8,128)} %copy.71.x_ref), custom_call_target="tpu_custom_call" | custom-call | tf_op jit(solution)/shard_map/pallas_call | solution.py:103
  414.5 2.5 fusion.65
  417.0 2.6 fusion.102
  422.5 8.9 %while.43 = (s32[]{:T(128)}, f32[2,64,1024]{2,1,0:T(8,128)S(1)}, s32[2,1024]{1,0:T(2,128)S(1)}, f32[64,2048]{1,0:T(8,128)S(1)}, s32[]{:T(128)}) while((s32[]{:T(128)}, f32[2,64,1024]{2,1,0:T(8,128)S(1)}, s32[2,1024]{1,0:T(2,128)S(1)}, f32[64,2048]{1,0:T(8,128)S(1)}, s32[]{:T(128)}) %tuple.109), condition=%wide.region_10.11_spmd, body=%wide.region_9.10_spmd.sunk | while | flops 1612709888 | bytes 798797 | solution.py:215
  422.5 4.4 fusion.178
  427.0 4.4 fusion.178
  435.2 2.6 fusion.62
  437.7 1.9 fusion.101
  446.8 5.7 fusion.21
  452.6 3.3 copy-done.1
  455.9 2.5 fusion.95
  458.4 1.8 fusion.106
  460.2 2.1 convolution_bitcast_fusion.13
  462.3 88.2 %scatter_custom_fusion.2 = f32[64,2560]{0,1:T(8,128)S(1)} fusion(s32[16384]{0:T(1024)S(1)} %bitcast.256, f32[16384,64]{1,0:T(8,128)} %bitcast.241, f32[]{:T(128)} %constant.20.clone.1), kind=kCustom, calls=%fused_computation.85 | custom fusion | flops 1048576 | bytes 655872 | tf_op jit(solution)/shard_map/transpose(jvp())/scatter-add | solution.py:142
  550.5 2.2 fusion.105
  556.7 29.4 %shard_map.258 = f32[64,1024]{1,0:T(8,128)} custom-call(f32[64,1024]{1,0:T(8,128)} %reshape.220.x_ref), custom_call_target="tpu_custom_call" | custom-call | tf_op jit(solution)/shard_map/pallas_call | solution.py:103
  587.9 1.8 fusion.33
  589.7 2.3 collective-permute-start.4
  592.0 3.1 collective-permute-start.7
  596.4 3.6 collective-permute-start.5
  606.9 3.7 scatter_fusion
  (175 shorter events, 60.6 us)
Async XLA Ops:
  0.6 147.8 %copy-start = (f32[64,64]{1,0:T(8,128)S(1)}, f32[64,64]{1,0:T(8,128)}, u32[]{:S(2)}) copy-start(f32[64,64]{1,0:T(8,128)} %param.37) | copy-start | bytes 49156
  3.9 25.5 %collective-permute-start.3 = (f32[64,128]{1,0:T(8,128)S(1)}, f32[64,128]{1,0:T(8,128)S(1)}, u32[]{:S(2)}, u32[]{:S(2)}) collective-permute-start(f32[64,128]{1,0:T(8,128)S(1)} %get-tuple-element.220), channel_id=1, source_target_pairs={{1,0},{2,1},{3,2},{4,3},{5,4},{6,5},{7,6},{8,7},{9,8},{10,9},{11,1... | collective-permute-start | bytes 98312 | tf_op jit(solution)/shard_map/ppermute | solution.py:123
  5.2 24.2 %collective-permute-start.2 = (f32[64,128]{1,0:T(8,128)S(1)}, f32[64,128]{1,0:T(8,128)S(1)}, u32[]{:S(2)}, u32[]{:S(2)}) collective-permute-start(f32[64,128]{1,0:T(8,128)S(1)} %get-tuple-element.221), channel_id=1, source_target_pairs={{0,1},{1,2},{2,3},{3,4},{4,5},{5,6},{6,7},{7,8},{8,9},{9,10},{10,1... | collective-permute-start | bytes 98312 | tf_op jit(solution)/shard_map/ppermute | solution.py:123
  10.2 19.2 %collective-permute-start.1 = (f32[64,128]{1,0:T(8,128)S(1)}, f32[64,128]{1,0:T(8,128)S(1)}, u32[]{:S(2)}, u32[]{:S(2)}) collective-permute-start(f32[64,128]{1,0:T(8,128)S(1)} %get-tuple-element.222), channel_id=1, source_target_pairs={{32,0},{64,32},{96,64},{128,96},{160,128},{192,160},{224,192},{33,... | collective-permute-start | bytes 98312 | tf_op jit(solution)/shard_map/ppermute | solution.py:123
  14.9 14.4 %collective-permute-start = (f32[64,128]{1,0:T(8,128)S(1)}, f32[64,128]{1,0:T(8,128)S(1)}, u32[]{:S(2)}, u32[]{:S(2)}) collective-permute-start(f32[64,128]{1,0:T(8,128)S(1)} %get-tuple-element.223), channel_id=1, source_target_pairs={{0,32},{32,64},{64,96},{96,128},{128,160},{160,192},{192,224},{1,3... | collective-permute-start | bytes 98312 | tf_op jit(solution)/shard_map/ppermute | solution.py:123
  24.3 62.6 %copy-start.3 = (f32[64,2048]{0,1:T(8,128)}, f32[64,2048]{0,1:T(8,128)S(1)}, u32[]{:S(2)}) copy-start(f32[64,2048]{0,1:T(8,128)S(1)} %fusion.81) | copy-start | bytes 1572868
  29.5 0.8 copy-start.5
  86.8 4.9 copy-start.22
  86.8 7.0 %copy-start.18 = (f32[64,128]{1,0:T(8,128)S(1)}, f32[64,128]{1,0:T(8,128)}, u32[]{:S(2)}) copy-start(f32[64,128]{1,0:T(8,128)} %param.34) | copy-start | bytes 98308
  86.8 7.6 %copy-start.2 = (f32[64,2048]{1,0:T(8,128)S(1)}, f32[64,2048]{1,0:T(8,128)}, u32[]{:S(2)}) copy-start(f32[64,2048]{1,0:T(8,128)} %param.25) | copy-start | bytes 1572868
  86.8 9.1 %copy-start.32 = (f32[64,64]{1,0:T(8,128)S(1)}, f32[64,64]{1,0:T(8,128)}, u32[]{:S(2)}) copy-start(f32[64,64]{1,0:T(8,128)} %param.35) | copy-start | bytes 49156
  86.8 9.9 %copy-start.16 = (f32[64,2048]{1,0:T(8,128)S(1)}, f32[64,2048]{1,0:T(8,128)}, u32[]{:S(2)}) copy-start(f32[64,2048]{1,0:T(8,128)} %custom-call) | copy-start | bytes 1572868
  93.0 0.8 copy-start.7
  95.0 0.8 copy-start.15
  96.6 47.9 %copy-start.9 = (f32[64,2048]{1,0:T(8,128)}, f32[64,2048]{1,0:T(8,128)S(1)}, u32[]{:S(2)}) copy-start(f32[64,2048]{1,0:T(8,128)S(1)} %fusion.39) | copy-start | bytes 1572868
  96.7 47.9 %copy-start.19 = (f32[64,128]{1,0:T(8,128)S(1)}, f32[64,128]{1,0:T(8,128)}, u32[]{:S(2)}) copy-start(f32[64,128]{1,0:T(8,128)} %param.39) | copy-start | bytes 98308
  96.7 49.3 %copy-start.21 = (f32[64,64]{1,0:T(8,128)S(1)}, f32[64,64]{1,0:T(8,128)}, u32[]{:S(2)}) copy-start(f32[64,64]{1,0:T(8,128)} %param.36) | copy-start | bytes 49156
  103.7 138.7 %copy-start.20 = (f32[64,64]{1,0:T(8,128)S(1)}, f32[64,64]{1,0:T(8,128)}, u32[]{:S(2)}) copy-start(f32[64,64]{1,0:T(8,128)} %param.38) | copy-start | bytes 49156
  147.6 0.8 copy-start.17
  244.6 15.5 %copy-start.29 = (f32[64,64]{1,0:T(8,128)S(1)}, f32[64,64]{1,0:T(8,128)}, u32[]{:S(2)}) copy-start(f32[64,64]{1,0:T(8,128)} %param.40) | copy-start | bytes 49156
  255.6 8.3 %copy-start.10 = (f32[64,2048]{1,0:T(8,128)S(1)}, f32[64,2048]{1,0:T(8,128)}, u32[]{:S(2)}) copy-start(f32[64,2048]{1,0:T(8,128)} %copy-done.9) | copy-start | bytes 1572868
  279.3 140.3 %copy-start.11 = (f32[64,2048]{1,0:T(8,128)S(1)}, f32[64,2048]{1,0:T(8,128)}, u32[]{:S(2)}) copy-start(f32[64,2048]{1,0:T(8,128)} %shard_map.256) | copy-start | bytes 1572868
  422.5 15.3 %copy-start.33 = (f32[64,64]{1,0:T(8,128)S(1)}, f32[64,64]{1,0:T(8,128)}, u32[]{:S(2)}) copy-start(f32[64,64]{1,0:T(8,128)} %param.35) | copy-start | bytes 49156
  431.4 0.8 copy-start.12
  432.2 7.4 %copy-start.8 = (f32[2048,64]{0,1:T(8,128)S(1)}, f32[2048,64]{0,1:T(8,128)}, u32[]{:S(2)}) copy-start(f32[2048,64]{0,1:T(8,128)} %copy-done.7) | copy-start | bytes 1572868
  432.2 14.6 %copy-start.4 = (f32[64,2048]{0,1:T(8,128)S(1)}, f32[64,2048]{0,1:T(8,128)}, u32[]{:S(2)}) copy-start(f32[64,2048]{0,1:T(8,128)} %copy-done.3) | copy-start | bytes 1572868
  435.1 5.7 copy-start.13
  452.6 3.3 copy-start.1
  455.8 4.4 copy-start.14
  455.8 94.7 %copy-start.6 = (f32[64,2560]{1,0:T(8,128)S(1)}, f32[64,2560]{1,0:T(8,128)}, u32[]{:S(2)}) copy-start(f32[64,2560]{1,0:T(8,128)} %copy-done.5) | copy-start | bytes 1966084
  455.8 99.5 %copy-start.27 = (f32[64,64]{1,0:T(8,128)S(1)}, f32[64,64]{1,0:T(8,128)}, u32[]{:S(2)}) copy-start(f32[64,64]{1,0:T(8,128)} %fusion.55) | copy-start | bytes 49156
  455.8 99.6 %copy-start.30 = (f32[64,64]{1,0:T(8,128)S(1)}, f32[64,64]{1,0:T(8,128)}, u32[]{:S(2)}) copy-start(f32[64,64]{1,0:T(8,128)} %fusion.62) | copy-start | bytes 49156
  455.8 99.6 %copy-start.28 = (f32[64,64]{1,0:T(8,128)S(1)}, f32[64,64]{1,0:T(8,128)}, u32[]{:S(2)}) copy-start(f32[64,64]{1,0:T(8,128)} %fusion.107) | copy-start | bytes 49156
  455.9 99.9 %copy-start.25 = (f32[64,64]{1,0:T(8,128)S(1)}, f32[64,64]{1,0:T(8,128)}, u32[]{:S(2)}) copy-start(f32[64,64]{1,0:T(8,128)} %fusion.108) | copy-start | bytes 49156
  455.9 99.9 %copy-start.26 = (f32[64,64]{1,0:T(8,128)S(1)}, f32[64,64]{1,0:T(8,128)}, u32[]{:S(2)}) copy-start(f32[64,64]{1,0:T(8,128)} %fusion.109) | copy-start | bytes 49156
  455.9 100.0 %copy-start.23 = (f32[64,64]{1,0:T(8,128)S(1)}, f32[64,64]{1,0:T(8,128)}, u32[]{:S(2)}) copy-start(f32[64,64]{1,0:T(8,128)} %fusion.110) | copy-start | bytes 49156
  455.9 100.0 %copy-start.24 = (f32[64,64]{1,0:T(8,128)S(1)}, f32[64,64]{1,0:T(8,128)}, u32[]{:S(2)}) copy-start(f32[64,64]{1,0:T(8,128)} %fusion.111) | copy-start | bytes 49156
  458.4 142.7 %copy-start.31 = (f32[64]{0:T(128)S(1)}, f32[64]{0:T(128)}, u32[]{:S(2)}) copy-start(f32[64]{0:T(128)} %get-tuple-element.233) | copy-start | bytes 772
  589.7 17.0 %collective-permute-start.4 = (f32[64,128]{1,0:T(8,128)S(1)}, f32[64,128]{1,0:T(8,128)S(1)}, u32[]{:S(2)}, u32[]{:S(2)}) collective-permute-start(f32[64,128]{1,0:T(8,128)S(1)} %get-tuple-element.206), channel_id=1, source_target_pairs={{32,0},{64,32},{96,64},{128,96},{160,128},{192,160},{224,192},{33,... | collective-permute-start | bytes 98312 | tf_op jit(solution)/shard_map/ppermute | solution.py:123
  592.0 14.7 %collective-permute-start.7 = (f32[64,128]{1,0:T(8,128)S(1)}, f32[64,128]{1,0:T(8,128)S(1)}, u32[]{:S(2)}, u32[]{:S(2)}) collective-permute-start(f32[64,128]{1,0:T(8,128)S(1)} %get-tuple-element.207), channel_id=1, source_target_pairs={{0,1},{1,2},{2,3},{3,4},{4,5},{5,6},{6,7},{7,8},{8,9},{9,10},{10,1... | collective-permute-start | bytes 98312 | tf_op jit(solution)/shard_map/ppermute | solution.py:123
  595.1 11.6 %collective-permute-start.6 = (f32[64,128]{1,0:T(8,128)S(1)}, f32[64,128]{1,0:T(8,128)S(1)}, u32[]{:S(2)}, u32[]{:S(2)}) collective-permute-start(f32[64,128]{1,0:T(8,128)S(1)} %get-tuple-element.208), channel_id=1, source_target_pairs={{1,0},{2,1},{3,2},{4,3},{5,4},{6,5},{7,6},{8,7},{9,8},{10,9},{11,1... | collective-permute-start | bytes 98312 | tf_op jit(solution)/shard_map/ppermute | solution.py:123
  596.4 10.3 %collective-permute-start.5 = (f32[64,128]{1,0:T(8,128)S(1)}, f32[64,128]{1,0:T(8,128)S(1)}, u32[]{:S(2)}, u32[]{:S(2)}) collective-permute-start(f32[64,128]{1,0:T(8,128)S(1)} %get-tuple-element.209), channel_id=1, source_target_pairs={{0,32},{32,64},{64,96},{96,128},{128,160},{160,192},{192,224},{1,3... | collective-permute-start | bytes 98312 | tf_op jit(solution)/shard_map/ppermute | solution.py:123

commit v2 on v0

v2 whole, which is shorter than its diff:
```python
from functools import partial

import jax
import jax.numpy as jnp
from jax import lax
from jax.experimental import pallas as pl
from jax.experimental.pallas import tpu as pltpu
from jax.sharding import PartitionSpec as P

COARSE = 2048
EXT = 2560
RADIX = 256
SHIFT = 8
WIDTH = 2048
UNROLL = 1
VMEM_LIMIT = 56 * 2**20
PART = (16, 64, 128)
UPG = (2, 64, 128)
FG = (4, 64, 128)


def table_scratch():
    return ((EXT // RADIX * 64, 2 * RADIX), jnp.bfloat16)


def sums_scratch():
    return ((EXT // RADIX * 64, RADIX), jnp.float32)

MESH = pl.DeviceIdType.MESH


def halves(values):
    high = values.astype(jnp.bfloat16)
    return high, (values - high.astype(jnp.float32)).astype(jnp.bfloat16)


def product(left, right):
    left_high, left_low = halves(left)
    right_high, right_low = halves(right)
    return jnp.dot(jnp.concatenate([left_high, left_low, left_high], axis=1),
                   jnp.concatenate([right_high, right_high, right_low], axis=0),
                   preferred_element_type=jnp.float32)


def product_nt(left, right):
    left_high, left_low = halves(left)
    right_high, right_low = halves(right)
    return lax.dot_general(jnp.concatenate([left_high, left_low, left_high], axis=1),
                           jnp.concatenate([right_high, right_high, right_low], axis=1),
                           (((1,), (1,)), ((), ())), preferred_element_type=jnp.float32)


def product_tn(left, right):
    return product(left.T, right)


def selector(index_row):
    rows = lax.broadcasted_iota(jnp.int32, (RADIX, index_row.shape[1]), 0).astype(jnp.bfloat16)
    low = (index_row & (RADIX - 1)).astype(jnp.float32).astype(jnp.bfloat16)
    return jnp.where(rows == low, jnp.bfloat16(1), jnp.bfloat16(0))


def fill_table(table_ref, values):
    high, low = halves(values)
    for block in range(values.shape[1] // RADIX):
        columns = slice(block * RADIX, (block + 1) * RADIX)
        table_ref[block * 64:block * 64 + 64, :RADIX] = high[:, columns]
        table_ref[block * 64:block * 64 + 64, RADIX:] = low[:, columns]


def read_table(table_ref, blocks, index_row):
    picked = selector(index_row)
    found = jnp.dot(table_ref[:blocks * 64], jnp.concatenate([picked, picked], axis=0),
                    preferred_element_type=jnp.float32)
    chosen = jnp.broadcast_to(index_row >> SHIFT, (64, index_row.shape[1]))
    total = found[:64]
    for block in range(1, blocks):
        total = jnp.where(chosen == block, found[block * 64:block * 64 + 64], total)
    return total


def spread(values, blocks, index_row, low_column):
    high, low = halves(values)
    chosen = jnp.broadcast_to(index_row >> SHIFT, (64, index_row.shape[1]))
    parts = []
    for block in range(blocks):
        mask = jnp.where(chosen == block, 1.0, 0.0).astype(jnp.bfloat16)
        parts.append(jnp.concatenate([high * mask, low * mask], axis=1))
    lanes = lax.broadcasted_iota(jnp.int32, (low_column.shape[0], RADIX), 1).astype(jnp.bfloat16)
    picked = jnp.where(lanes == low_column.astype(jnp.bfloat16), jnp.bfloat16(1), jnp.bfloat16(0))
    return jnp.dot(jnp.concatenate(parts, axis=0), jnp.concatenate([picked, picked], axis=0),
                   preferred_element_type=jnp.float32)


def fill_columns(columns, rows):
    count = rows.shape[0]
    if count < 8:
        rows = jnp.concatenate([rows] * (8 // count), axis=0)
    turned = (rows & (RADIX - 1)).astype(jnp.float32).T
    for step in range(count):
        columns[step] = turned[:, step:step + 1]


def gathered_sums(sums_ref, blocks):
    return jnp.concatenate([sums_ref[block * 64:block * 64 + 64] for block in range(blocks)], axis=1)


def span(position, size):
    return pl.ds(pl.multiple_of(position * size, size), size)


def read_all(out_ref, table_ref, index_ref, width):
    def body(step, carry):
        part = span(step, width)
        out_ref[:, part] = read_table(table_ref, COARSE // RADIX, index_ref[:, part])
        return carry
    lax.fori_loop(0, index_ref.shape[1] // width, body, 0)


def spread_all(columns, values, index_row):
    blocks = COARSE // RADIX
    fill_columns(columns, index_row)
    found = spread(values, blocks, index_row, columns[0])
    return jnp.concatenate([found[block * 64:block * 64 + 64] for block in range(blocks)], axis=1)


def mix_all(sums_ref, table_ref, columns, edges_ref, sender, receiver):
    blocks = COARSE // RADIX
    sums_ref[:blocks * 64] = jnp.zeros((blocks * 64, RADIX), jnp.float32)
    fill_columns(columns, jnp.concatenate(
        [edges_ref[receiver:receiver + 1, step * 2048:step * 2048 + 2048] for step in range(4)], axis=0))

    def body(step, carry):
        part = span(step, 2048)
        found = read_table(table_ref, blocks, edges_ref[sender:sender + 1, part])
        sums_ref[:blocks * 64] += spread(found, blocks, edges_ref[receiver:receiver + 1, part], columns[step])
        return carry
    lax.fori_loop(0, 4, body, 0)
    return gathered_sums(sums_ref, blocks)


def extended(features, halo):
    return jnp.concatenate([features] + [halo[slot] for slot in range(4)], axis=1)


def put_slabs(out, values):
    for position in range(16):
        out[position] = values[:, position * 128:position * 128 + 128]


def gate(values):
    return 1.0 / (1.0 + jnp.exp(-values))


def silu_and_slope(values):
    opened = gate(values)
    silu = values * opened
    return silu, opened + silu * (1.0 - opened)


def fine_forward_kernel(scale, features, halo, sources, to_coarse, edge_in, edge_out, node_in, node_out, bias,
                        middle, slope, hidden, node_pre, pooled, table, received, sums, columns):
    feats = features[...]
    weights = edge_in[...]
    received[...] = product(weights[:, :64], feats) + bias[:, 0:1]
    fill_table(table, product(weights[:, 64:], extended(feats, halo)))

    def body(step, carry):
        part = span(step, WIDTH)
        base = received[:, part]

        def edge(k, total):
            silu, slopes = silu_and_slope(base + read_table(table, EXT // RADIX, sources[pl.ds(k, 1), part]))
            slope[k, :, part] = slopes
            return total + silu
        hidden[:, part] = lax.fori_loop(0, 8, edge, jnp.zeros((64, WIDTH), jnp.float32), unroll=UNROLL)
        return carry
    lax.fori_loop(0, 2048 // WIDTH, body, 0)
    aggregate = product(edge_out[...], hidden[...])
    pre = product(node_in[...], jnp.concatenate([feats, aggregate], axis=0)) + bias[:, 1:2]
    node_pre[...] = pre
    middle[...] = feats + product(node_out[...], pre * gate(pre))
    put_slabs(pooled, spread_all(columns, middle[...], to_coarse[...]) * scale)


def coarse_kernel(factor, pooled, coarse_in, coarse_out, coarse_mix, bias, edges, to_fine, middle, cotangent,
                  up_in, up_out, output, grad_middle, grad_mixed, mixed_sum, up_grads, table, looked, sums, columns):
    values = pooled[...]
    pre = product(coarse_in[...], values) + bias[:, 2:3]
    nodes = values + product(coarse_out[...], pre * gate(pre))
    fill_table(table, nodes)
    summed = mix_all(sums, table, columns, edges, 0, 1)
    mixed_sum[...] = summed
    fill_table(table, nodes + product(coarse_mix[...], summed) * factor)
    read_all(looked, table, to_fine, WIDTH)
    both = jnp.concatenate([middle[...], looked[...]], axis=0)
    silu, slopes = silu_and_slope(product(up_in[...], both) + bias[:, 3:4])
    output[...] = middle[...] + product(up_out[...], silu)
    cot = cotangent[...]
    grad_pre = product_tn(up_out[...], cot) * slopes
    up_grads[0] = product_nt(grad_pre, both)
    up_grads[1] = jnp.concatenate(
        [product_nt(cot, silu), jnp.broadcast_to(jnp.sum(grad_pre, axis=1, keepdims=True), (64, 64))], axis=1)
    grad_both = product_tn(up_in[...], grad_pre)
    grad_middle[...] = cot + grad_both[:64]
    put_slabs(grad_mixed, spread_all(columns, grad_both[64:], to_fine[...]))


def backward_kernel(factor, scale, grad_mixed, mixed_sum, pooled, coarse_in, coarse_out, coarse_mix, bias, edges,
                    to_coarse, grad_middle, node_pre, hidden, slope, features, halo, sources, edge_in, edge_out,
                    node_in, node_out, own, grad_halo, fine_grads, coarse_grads, table, found, scratch, sums, columns):
    grad_mix_all = grad_mixed[...]
    coarse_grads[:, 256:384] = jnp.concatenate(
        [product_nt(grad_mix_all, mixed_sum[...]) * factor, jnp.zeros((64, 64), jnp.float32)], axis=1)
    fill_table(table, product_tn(coarse_mix[...], grad_mix_all) * factor)
    grad_nodes = grad_mix_all + mix_all(sums, table, columns, edges, 1, 0)
    values = pooled[...]
    silu, slopes = silu_and_slope(product(coarse_in[...], values) + bias[:, 2:3])
    grad_pre = product_tn(coarse_out[...], grad_nodes) * slopes
    coarse_grads[:, 0:128] = jnp.concatenate([product_nt(grad_pre, values), product_nt(grad_nodes, silu)], axis=1)
    coarse_grads[:, 128:256] = jnp.broadcast_to(jnp.sum(grad_pre, axis=1, keepdims=True), (64, 128))
    fill_table(table, grad_nodes + product_tn(coarse_in[...], grad_pre))
    read_all(found, table, to_coarse, WIDTH)
    grad_mid = grad_middle[...] + found[...] * scale
    feats = features[...]
    silu, slopes = silu_and_slope(node_pre[...])
    aggregate = product(edge_out[...], hidden[...])
    grad_pre = product_tn(node_out[...], grad_mid) * slopes
    fine_grads[0] = product_nt(grad_pre, jnp.concatenate([feats, aggregate], axis=0))
    node_bias = jnp.sum(grad_pre, axis=1, keepdims=True)
    grad_both = product_tn(node_in[...], grad_pre)
    grad_sum = grad_both[64:]
    fine_grads[1] = jnp.concatenate(
        [product_nt(grad_mid, silu), product_nt(grad_sum, hidden[...])], axis=1)
    found[...] = grad_mid + grad_both[:64]
    scratch[...] = product_tn(edge_out[...], grad_sum)
    blocks = EXT // RADIX
    sums[...] = jnp.zeros(sums.shape, jnp.float32)
    fill_columns(columns, sources[...])

    def body(step, carry):
        part = span(step, WIDTH)
        base = scratch[:, part]

        def edge(k, total):
            grad_edge = base * slope[k, :, part]
            sums[...] += spread(grad_edge, blocks, sources[pl.ds(k, 1), part], columns[k, part])
            return total + grad_edge
        scratch[:, part] = lax.fori_loop(0, 8, edge, jnp.zeros((64, WIDTH), jnp.float32), unroll=UNROLL)
        return carry
    lax.fori_loop(0, 2048 // WIDTH, body, 0)
    grad_sent = gathered_sums(sums, blocks)
    grad_received = scratch[...]
    fine_grads[2] = jnp.concatenate(
        [product_nt(grad_received, feats),
         product_nt(grad_sent, extended(feats, halo))], axis=1)
    fine_grads[3] = jnp.concatenate(
        [jnp.broadcast_to(jnp.sum(grad_received, axis=1, keepdims=True), (64, 64)),
         jnp.broadcast_to(node_bias, (64, 64))], axis=1)
    weights = edge_in[...]
    back = product_tn(weights[:, 64:], grad_sent)
    own[...] = found[...] + product_tn(weights[:, :64], grad_received) + back[:, :2048]
    for slot in range(4):
        grad_halo[slot] = back[:, 2048 + slot * 128:2048 + slot * 128 + 128]


def call(kernel, outs, scratch, *operands):
    return pl.pallas_call(
        kernel,
        out_shape=[jax.ShapeDtypeStruct(shape, jnp.float32) for shape in outs],
        in_specs=[pl.BlockSpec(memory_space=pltpu.VMEM)] * len(operands),
        out_specs=[pl.BlockSpec(memory_space=pltpu.VMEM)] * len(outs),
        scratch_shapes=[pltpu.VMEM(shape, dtype) for shape, dtype in scratch],
        compiler_params=pltpu.CompilerParams(vmem_limit_bytes=VMEM_LIMIT),
    )(*operands)


def copy_to(source, target, sent, arrived, device):
    return pltpu.make_async_remote_copy(
        src_ref=source, dst_ref=target, send_sem=sent, recv_sem=arrived, device_id=device, device_id_type=MESH)


def each(make, count, action):
    def body(k, carry):
        getattr(make(k), action)()
        return carry
    lax.fori_loop(1, count, body, 0)


def side_devices(back):
    gx, gy = lax.axis_index("gx"), lax.axis_index("gy")
    up, down = (lax.rem(gx + 1, 8), gy), (lax.rem(gx + 7, 8), gy)
    right, left = (gx, lax.rem(gy + 1, 32)), (gx, lax.rem(gy + 31, 32))
    return (down, up, left, right) if back else (up, down, right, left)


def side_exists(back):
    gx, gy = lax.axis_index("gx"), lax.axis_index("gy")
    below = (gx > 0, gx < 7, gy > 0, gy < 31)
    return (below[1], below[0], below[3], below[2]) if back else below


def greet_sides(barrier):
    for device in side_devices(False):
        pl.semaphore_signal(barrier, inc=1, device_id=device, device_id_type=MESH)


class WholeSum:
    def __init__(self, slabs, x_ref, scratch):
        (self.half, self.core_parts, self.flat_parts, self.piece, self.line_parts, self.half_out, self.other,
         self.core_sems, self.flat_sent, self.flat_arrived, self.line_sent, self.line_arrived,
         self.back_sent, self.back_arrived) = scratch
        self.slabs, self.rows, self.x_ref = slabs, 2 * slabs, x_ref
        gx, gy = lax.axis_index("gx"), lax.axis_index("gy")
        self.core, self.z = lax.rem(gx, 2), lax.rem(gy, 8)
        self.flat = gx // 2 * 4 + gy // 8
        self.gx, self.gy = gx, gy
        self.sibling = (gx + 1 - 2 * self.core, gy)

    def flat_device(self, place):
        return (place // 4 * 2 + self.core, lax.rem(place, 4) * 8 + self.z)

    def line_device(self, z):
        return (self.gx, self.gy - self.z + z)

    def flat_place(self, k):
        return lax.rem(self.flat + k, 16)

    def chunk(self, ref, place):
        start = place * self.rows
        return ref.at[start // 32, pl.ds(pl.multiple_of(lax.rem(start, 32), 16), self.rows)]

    def own_rows(self, core):
        return pl.ds(pl.multiple_of(core * 32, 32), 32)

    def greet(self, barrier):
        pl.semaphore_signal(barrier, inc=1, device_id=self.sibling, device_id_type=MESH)

        def flat(k, carry):
            pl.semaphore_signal(barrier, inc=1, device_id=self.flat_device(self.flat_place(k)), device_id_type=MESH)
            return carry

        def line(k, carry):
            pl.semaphore_signal(barrier, inc=1, device_id=self.line_device(lax.rem(self.z + k, 8)),
                                device_id_type=MESH)
            return carry
        lax.fori_loop(1, 16, flat, 0)
        lax.fori_loop(1, 8, line, 0)
        return 23

    def to_core(self):
        return copy_to(self.x_ref.at[:, self.own_rows(1 - self.core)], self.core_parts,
                       self.core_sems.at[0], self.core_sems.at[1], self.sibling)

    def to_flat(self, k):
        place = self.flat_place(k)
        return copy_to(self.chunk(self.half, place), self.flat_parts.at[k], self.flat_sent.at[k],
                       self.flat_arrived.at[k], self.flat_device(place))

    def to_line(self, k):
        return copy_to(self.piece, self.line_parts.at[self.z], self.line_sent.at[k], self.line_arrived.at[k],
                       self.line_device(lax.rem(self.z + k, 8)))

    def back_flat(self, k):
        mine = self.chunk(self.half_out, self.flat)
        return copy_to(mine, mine, self.back_sent.at[k], self.back_arrived.at[k],
                       self.flat_device(self.flat_place(k)))

    def back_core(self):
        return copy_to(self.half_out, self.other, self.core_sems.at[2], self.core_sems.at[3], self.sibling)

    def run(self, beside=None):
        self.to_core().start()
        if beside is not None:
            beside()
        self.to_core().wait()
        self.half[...] = self.x_ref[:, self.own_rows(self.core)] + self.core_parts[...]
        each(self.to_flat, 16, "start")
        each(self.to_flat, 16, "wait")
        total = self.chunk(self.half, self.flat)[...]
        for k in range(1, 16):
            total = total + self.flat_parts[k]
        self.piece[...] = total
        each(self.to_line, 8, "start")
        self.line_parts[self.z] = total
        each(self.to_line, 8, "wait")
        total = self.line_parts[0]
        for k in range(1, 8):
            total = total + self.line_parts[k]
        self.chunk(self.half_out, self.flat)[...] = total
        each(self.back_flat, 16, "start")
        each(self.back_flat, 16, "wait")
        self.back_core().start()
        self.back_core().wait()

    def slab(self, position):
        first = jnp.broadcast_to(self.core == 0, (32, 128))
        own, other = self.half_out[position], self.other[position]
        return jnp.concatenate([jnp.where(first, own, other), jnp.where(first, other, own)], axis=0)


def sum_scratch(slabs):
    rows, dma = 2 * slabs, pltpu.SemaphoreType.DMA
    half = pltpu.VMEM((slabs, 32, 128), jnp.float32)
    return [half, half, pltpu.VMEM((16, rows, 128), jnp.float32), pltpu.VMEM((rows, 128), jnp.float32),
            pltpu.VMEM((8, rows, 128), jnp.float32), half, half,
            dma((4,)), dma((16,)), dma((16,)), dma((8,)), dma((8,)), dma((16,)), dma((16,))]


def remote_call(kernel, outs, scratch, collective_id, *operands):
    return pl.pallas_call(
        kernel,
        out_shape=[jax.ShapeDtypeStruct(shape, jnp.float32) for shape in outs],
        in_specs=[pl.BlockSpec(memory_space=pltpu.VMEM)] * len(operands),
        out_specs=[pl.BlockSpec(memory_space=pltpu.VMEM)] * len(outs),
        scratch_shapes=scratch,
        compiler_params=pltpu.CompilerParams(collective_id=collective_id, has_side_effects=True,
                                             vmem_limit_bytes=VMEM_LIMIT),
    )(*operands)


def add_up_kernel(x_ref, o_ref, *scratch):
    summing = WholeSum(16, x_ref, scratch)
    barrier = pltpu.get_barrier_semaphore()
    pl.semaphore_wait(barrier, summing.greet(barrier))
    summing.run()
    for position in range(16):
        o_ref[:, position * 128:position * 128 + 128] = summing.slab(position)


def add_up(table):
    total, = remote_call(add_up_kernel, [(64, 2048)], sum_scratch(16), 0, table)
    return total


def side_copy(packets, arrived_ref, sent, arrived, slot, back):
    return copy_to(packets.at[slot], arrived_ref.at[slot], sent.at[slot], arrived.at[slot], side_devices(back)[slot])


def halo_kernel(features, rows, halo, table, packets, arrived_ref, sent, arrived):
    barrier = pltpu.get_barrier_semaphore()
    greet_sides(barrier)
    fill_table(table, features[...])
    for slot in range(4):
        packets[slot] = read_table(table, COARSE // RADIX, rows[slot:slot + 1, :])
    pl.semaphore_wait(barrier, 4)
    for slot in range(4):
        side_copy(packets, arrived_ref, sent, arrived, slot, False).start()
    for slot in range(4):
        side_copy(packets, arrived_ref, sent, arrived, slot, False).wait()
        there = jnp.broadcast_to(side_exists(False)[slot], (64, 128))
        halo[slot] = jnp.where(there, arrived_ref[slot], 0.0)


def exchange(features, rows):
    dma = pltpu.SemaphoreType.DMA
    slots = pltpu.VMEM((4, 64, 128), jnp.float32)
    halo, = remote_call(
        halo_kernel, [(4, 64, 128)],
        [pltpu.VMEM((COARSE // RADIX * 64, 2 * RADIX), jnp.bfloat16), slots, slots, dma((4,)), dma((4,))],
        1, features, rows)
    return halo


def final_kernel(own, grad_halo, rows, fine_grads, up_grads, coarse_grads, grad_features, grad_edge_in,
                 grad_edge_out, grad_node_in, grad_node_out, grad_up_in, grad_up_out, grad_biases,
                 packed, arrived_ref, sent, arrived, *scratch):
    summing = WholeSum(8, packed, scratch)
    barrier = pltpu.get_barrier_semaphore()
    count = summing.greet(barrier)
    greet_sides(barrier)
    packed[0:4] = fine_grads[...]
    packed[4:6] = up_grads[...]
    packed[6:8] = jnp.zeros((2, 64, 128), jnp.float32)
    pl.semaphore_wait(barrier, count + 4)
    for slot in range(4):
        side_copy(grad_halo, arrived_ref, sent, arrived, slot, True).start()

    def add_returned():
        columns, parts = [], []
        for slot in range(4):
            side_copy(grad_halo, arrived_ref, sent, arrived, slot, True).wait()
            there = jnp.broadcast_to(side_exists(True)[slot], (64, 128))
            parts.append(jnp.where(there, arrived_ref[slot], 0.0))
        indices = rows[...]
        lows = (jnp.concatenate([indices, indices], axis=0) & (RADIX - 1)).astype(jnp.float32).T
        index_row = jnp.concatenate([indices[slot:slot + 1, :] for slot in range(4)], axis=1)
        low_column = jnp.concatenate([lows[:, slot:slot + 1] for slot in range(4)], axis=0)
        blocks = COARSE // RADIX
        found = spread(jnp.concatenate(parts, axis=1), blocks, index_row, low_column)
        for block in range(blocks):
            part = slice(block * RADIX, (block + 1) * RADIX)
            grad_features[:, part] = own[:, part] + found[block * 64:block * 64 + 64]
    summing.run(add_returned)
    grad_node_in[...] = summing.slab(0)
    pair = summing.slab(1)
    grad_node_out[...] = pair[:, :64]
    grad_edge_out[...] = pair[:, 64:]
    grad_edge_in[...] = summing.slab(2)
    grad_up_in[...] = summing.slab(4)
    last = summing.slab(5)
    grad_up_out[...] = last[:, :64]
    fine_bias, up_bias, coarse_bias = summing.slab(3).T, last.T, coarse_grads[:, 128:256].T
    grad_biases[...] = jnp.concatenate(
        [fine_bias[0:1], fine_bias[64:65], coarse_bias[0:1], up_bias[64:65]], axis=0)


def local(
    features,
    cotangent,
    edge_src,
    send_rows,
    fine_to_coarse,
    coarse_to_fine,
    coarse_edges,
    edge_in,
    edge_out,
    node_in,
    node_out,
    coarse_in,
    coarse_out,
    coarse_mix,
    up_in,
    up_out,
    biases,
):
    scale = (COARSE / (features.shape[1] * lax.axis_size("gx") * lax.axis_size("gy"))) ** 0.5
    factor = (COARSE / coarse_edges.shape[1]) ** 0.5
    bias = biases.T
    to_coarse, to_fine = fine_to_coarse.reshape(1, -1), coarse_to_fine.reshape(1, -1)
    table, sums, columns = table_scratch(), sums_scratch(), ((8, 2048, 1), jnp.float32)
    wide = ((64, 2048), jnp.float32)
    halo = exchange(features, send_rows)
    middle, slope, hidden, node_pre, pooled_part = call(
        partial(fine_forward_kernel, scale),
        [(64, 2048), (8, 64, 2048), (64, 2048), (64, 2048), PART],
        [table, wide, sums, columns],
        features, halo, edge_src, to_coarse, edge_in, edge_out, node_in, node_out, bias)
    pooled = add_up(pooled_part)
    output, grad_middle, grad_mixed_part, mixed_sum, up_grads = call(
        partial(coarse_kernel, factor),
        [(64, 2048), (64, 2048), PART, (64, 2048), UPG],
        [table, wide, sums, columns],
        pooled, coarse_in, coarse_out, coarse_mix, bias, coarse_edges, to_fine, middle, cotangent, up_in, up_out)
    grad_mixed = add_up(grad_mixed_part)
    own, grad_halo, fine_grads, coarse_grads = call(
        partial(backward_kernel, factor, scale),
        [(64, 2048), (4, 64, 128), FG, (64, 384)],
        [table, wide, wide, sums, columns],
        grad_mixed, mixed_sum, pooled, coarse_in, coarse_out, coarse_mix, bias, coarse_edges, to_coarse,
        grad_middle, node_pre, hidden, slope, features, halo, edge_src, edge_in, edge_out, node_in, node_out)
    dma = pltpu.SemaphoreType.DMA
    (grad_features, grad_edge_in, grad_edge_out, grad_node_in, grad_node_out, grad_up_in, grad_up_out,
     grad_biases) = remote_call(
        final_kernel,
        [(64, 2048), (64, 128), (64, 64), (64, 128), (64, 64), (64, 128), (64, 64), (4, 64)],
        [pltpu.VMEM((8, 64, 128), jnp.float32), pltpu.VMEM((4, 64, 128), jnp.float32), dma((4,)), dma((4,)),
         *sum_scratch(8)],
        2, own, grad_halo, send_rows, fine_grads, up_grads, coarse_grads)
    return (
        output,
        grad_features,
        grad_edge_in,
        grad_edge_out,
        grad_node_in,
        grad_node_out,
        coarse_grads[:, 0:64],
        coarse_grads[:, 64:128],
        coarse_grads[:, 256:320],
        grad_up_in,
        grad_up_out,
        grad_biases,
    )


def solution(mesh):
    in_specs = (
        P(None, ("gx", "gy")),
        P(None, ("gx", "gy")),
        P(None, ("gx", "gy")),
        P(None, ("gx", "gy")),
        P(("gx", "gy")),
        P(("gx", "gy")),
        P(),
        P(),
        P(),
        P(),
        P(),
        P(),
        P(),
        P(),
        P(),
        P(),
        P(),
    )
    out_specs = (
        P(None, ("gx", "gy")),
        P(None, ("gx", "gy")),
        P(),
        P(),
        P(),
        P(),
        P(),
        P(),
        P(),
        P(),
        P(),
        P(),
    )
    return jax.shard_map(local, mesh=mesh, in_specs=in_specs, out_specs=out_specs, check_vma=False)
```

time: 1300 us -> 193 us (0.15); the launches traced: 1280 us -> 192 us
  waiting for transfers between devices: 743 us -> 0 us
  other arithmetic: 308 us -> 0 us
  Pallas kernels: 0 us -> 177 us
  matrix products: 101 us -> 0 us
  local copies, waits for them, and re-layouts: 93.4 us -> 14.3 us
  starting transfers between devices: 23.8 us -> 0 us
  between operations: 15 us -> 0.68 us
    psum x3 -> x0, waiting for transfers between devices: 743 us -> none  [the longest x2 500 us: coarse_total(): return lax.psum(table, ('gx', 'gy'))]
    scatter-add x4 -> x0, other arithmetic: 286 us -> none  [the longest x1 104 us: coarse_edge(): gathered = nodes[:, coarse_edges[0]]]
    pallas_call x0 -> x7, Pallas kernels: none -> 177 us  [the longest x4 96.3 us: remote_call(): pl.pallas_call(kernel, out_shape=[jax.ShapeDtypeStruct(shape, jnp.float32...]
    dot_general x44 -> x0, matrix products: 101 us -> none  [the longest x40 80.9 us: matmul(): jnp.dot(left_side, right_side, precision=lax.Precision.HIGHEST, preferred...]
    gather x3 -> x0, local copies, waits for them, and re-layouts: 55.9 us -> none  [the longest x1 54.7 us: fine_update(): sender_part[:, sources]]
    ppermute x8 -> x0, starting transfers between devices: 23.5 us -> none  [passed_along(): lax.ppermute(value, axis, [(source, source + steps) for source in range(l...]
  transfers between devices with their start and end apart: 11 -> 0, of which waited for: 3 -> 0; matrix products, arithmetic and copies ran while one was open for 2% -> 0% of each run, Pallas kernels for 0% -> 0%
where the time goes in v2:
time: 193 us; the launch traced here: 192 us
  Pallas kernels  177 us (92%)
  local copies, waits for them, and re-layouts  14.3 us (7%)
    pallas_call x4, Pallas kernels, remote_call(): pl.pallas_call(kernel, out_shape=[jax.ShapeDtypeStruct(shape, jnp.float32...  96.3 us
    pallas_call x3, Pallas kernels, call(): pl.pallas_call(kernel, out_shape=[jax.ShapeDtypeStruct(shape, jnp.float32...  80.4 us
    unnamed x9, local copies, waits for them, and re-layouts  12.8 us

profile of v2, /device:TPU:1, one launch (start us, length us, event | category | flops | bytes accessed | tf_op | source)
XLA Modules:
  0.0 191.7 jit_solution(15808838728750026595)
XLA Ops:
  0.6 1.4 copy.29
  2.0 14.6 %shard_map.256.halo = f32[4,64,128]{2,1,0:T(8,128)} custom-call(f32[64,2048]{1,0:T(8,128)} %features.5, s32[4,128]{1,0:T(4,128)} %rows.3), custom_call_target="tpu_custom_call" | custom-call | tf_op jit(solution)/shard_map/pallas_call | solution.py:411
  16.6 17.7 %shard_map.257 = (f32[64,2048]{1,0:T(8,128)}, f32[8,64,2048]{2,1,0:T(8,128)}, f32[64,2048]{1,0:T(8,128)}, f32[64,2048]{1,0:T(8,128)}, f32[16,64,128]{2,1,0:T(8,128)}) custom-call(f32[64,2048]{1,0:T(8,128)} %features.5, f32[4,64,128]{2,1,0:T(8,128)} %shard_map.256.halo, s32[8,2048]{1,0:T(8,128)} %sources.3, s32[1,2048]{1,0:T(1,128)} %bitcast.6, ...), custom_call_target="tpu_custom_call" | custom-call | tf_op jit(solution)/shard_map/pallas_call | solution.py:268
  34.4 27.3 %shard_map.258.pooled = f32[64,2048]{1,0:T(8,128)} custom-call(f32[16,64,128]{2,1,0:T(8,128)} %get-tuple-element.34.x_ref), custom_call_target="tpu_custom_call" | custom-call | tf_op jit(solution)/shard_map/pallas_call | solution.py:411
  61.7 24.4 %shard_map.259 = (f32[64,2048]{1,0:T(8,128)}, f32[64,2048]{1,0:T(8,128)}, f32[16,64,128]{2,1,0:T(8,128)}, f32[64,2048]{1,0:T(8,128)}, f32[2,64,128]{2,1,0:T(8,128)}) custom-call(f32[64,2048]{1,0:T(8,128)} %shard_map.258.pooled, f32[64,64]{1,0:T(8,128)} %coarse_in.3, f32[64,64]{1,0:T(8,128)} %coarse_out.3, f32[64,64]{1,0:T(8,128)} %coarse_mix.3, ...), custom_call_target="tpu_custom_call" | custom-call | tf_op jit(solution)/shard_map/pallas_call | solution.py:268
  86.1 27.3 %shard_map.260.grad_mixed = f32[64,2048]{1,0:T(8,128)} custom-call(f32[16,64,128]{2,1,0:T(8,128)} %get-tuple-element.37.x_ref), custom_call_target="tpu_custom_call" | custom-call | tf_op jit(solution)/shard_map/pallas_call | solution.py:411
  113.4 38.3 %shard_map.261 = (f32[64,2048]{1,0:T(8,128)}, f32[4,64,128]{2,1,0:T(8,128)}, f32[4,64,128]{2,1,0:T(8,128)}, f32[64,384]{1,0:T(8,128)}) custom-call(f32[64,2048]{1,0:T(8,128)} %shard_map.260.grad_mixed, f32[64,2048]{1,0:T(8,128)} %get-tuple-element.38.mixed_sum, f32[64,2048]{1,0:T(8,128)} %shard_map.258.pooled, f32[64,64]{1,0:T(8,128)} %coarse_in.3, ...), custom_call_target="tpu_custom_call" | custom-call | tf_op jit(solution)/shard_map/pallas_call | solution.py:268
  151.7 27.1 %shard_map.262 = (f32[64,2048]{1,0:T(8,128)}, f32[64,128]{1,0:T(8,128)}, f32[64,64]{1,0:T(8,128)}, f32[64,128]{1,0:T(8,128)}, f32[64,64]{1,0:T(8,128)}, /*index=...) custom-call(f32[64,2048]{1,0:T(8,128)} %get-tuple-element.43.own, f32[4,64,128]{2,1,0:T(8,128)} %get-tuple-element.44.grad_halo, ...), custom_call_target="tpu_custom_call" | custom-call | tf_op jit(solution)/shard_map/pallas_call | solution.py:411
  178.8 1.5 fusion
  180.3 1.9 copy.38
  182.2 1.4 copy.39
  183.6 1.4 copy.40
  184.9 1.4 copy.41
  186.3 1.4 copy.42
  187.7 1.4 copy.43
  189.0 1.4 copy.44
  190.4 1.3 copy.45

commit v3 on v2

v3 whole, which is shorter than its diff:
```python
from functools import partial

import jax
import jax.numpy as jnp
from jax import lax
from jax.experimental import pallas as pl
from jax.experimental.pallas import tpu as pltpu
from jax.sharding import PartitionSpec as P

COARSE = 2048
EXT = 2560
RADIX = 256
SHIFT = 8
WIDTH = 2048
VMEM_LIMIT = 56 * 2**20


MESH = pl.DeviceIdType.MESH


def halves(values):
    high = values.astype(jnp.bfloat16)
    return high, (values - high.astype(jnp.float32)).astype(jnp.bfloat16)


def product(left, right):
    left_high, left_low = halves(left)
    right_high, right_low = halves(right)
    return jnp.dot(jnp.concatenate([left_high, left_low, left_high], axis=1),
                   jnp.concatenate([right_high, right_high, right_low], axis=0),
                   preferred_element_type=jnp.float32)


def product_nt(left, right):
    left_high, left_low = halves(left)
    right_high, right_low = halves(right)
    return lax.dot_general(jnp.concatenate([left_high, left_low, left_high], axis=1),
                           jnp.concatenate([right_high, right_high, right_low], axis=1),
                           (((1,), (1,)), ((), ())), preferred_element_type=jnp.float32)


def product_tn(left, right):
    return product(left.T, right)


def selector(index_row):
    rows = lax.broadcasted_iota(jnp.int32, (RADIX, index_row.shape[1]), 0).astype(jnp.bfloat16)
    low = (index_row & (RADIX - 1)).astype(jnp.float32).astype(jnp.bfloat16)
    return jnp.where(rows == low, jnp.bfloat16(1), jnp.bfloat16(0))


def fill_table(table_ref, values):
    high, low = halves(values)
    for block in range(values.shape[1] // RADIX):
        columns = slice(block * RADIX, (block + 1) * RADIX)
        rows = slice(block * values.shape[0], (block + 1) * values.shape[0])
        table_ref[rows, :RADIX] = high[:, columns]
        table_ref[rows, RADIX:] = low[:, columns]


def read_table(table_ref, blocks, index_row, height=64):
    picked = selector(index_row)
    found = jnp.dot(table_ref[:blocks * height], jnp.concatenate([picked, picked], axis=0),
                    preferred_element_type=jnp.float32)
    chosen = jnp.broadcast_to(index_row >> SHIFT, (height, index_row.shape[1]))
    total = found[:height]
    for block in range(1, blocks):
        total = jnp.where(chosen == block, found[block * height:(block + 1) * height], total)
    return total


def spread(values, blocks, index_row, low_column):
    high, low = halves(values)
    chosen = jnp.broadcast_to(index_row >> SHIFT, (values.shape[0], index_row.shape[1]))
    parts = []
    for block in range(blocks):
        mask = jnp.where(chosen == block, 1.0, 0.0).astype(jnp.bfloat16)
        parts.append(jnp.concatenate([high * mask, low * mask], axis=1))
    lanes = lax.broadcasted_iota(jnp.int32, (low_column.shape[0], RADIX), 1).astype(jnp.bfloat16)
    picked = jnp.where(lanes == low_column.astype(jnp.bfloat16), jnp.bfloat16(1), jnp.bfloat16(0))
    return jnp.dot(jnp.concatenate(parts, axis=0), jnp.concatenate([picked, picked], axis=0),
                   preferred_element_type=jnp.float32)


def fill_columns(columns, rows):
    count = rows.shape[0]
    if count < 8:
        rows = jnp.concatenate([rows] * (8 // count), axis=0)
    turned = (rows & (RADIX - 1)).astype(jnp.float32).T
    for step in range(count):
        columns[step] = turned[:, step:step + 1]


def gathered_sums(sums_ref, blocks, height=64):
    return jnp.concatenate(
        [sums_ref[block * height:(block + 1) * height] for block in range(blocks)], axis=1)


def span(position, size):
    return pl.ds(pl.multiple_of(position * size, size), size)


def read_all(out_ref, table_ref, index_ref, width):
    def body(step, carry):
        part = span(step, width)
        out_ref[:, part] = read_table(table_ref, COARSE // RADIX, index_ref[:, part])
        return carry
    lax.fori_loop(0, index_ref.shape[1] // width, body, 0)


def spread_all(columns, values, index_row):
    blocks = COARSE // RADIX
    fill_columns(columns, index_row)
    found = spread(values, blocks, index_row, columns[0])
    return jnp.concatenate([found[block * 64:block * 64 + 64] for block in range(blocks)], axis=1)


def mix_half(sums_ref, table_ref, columns, edges_ref, sender, receiver, values):
    blocks = COARSE // RADIX
    used = blocks * 32
    fill_table(table_ref, values)
    sums_ref[:used] = jnp.zeros((used, RADIX), jnp.float32)
    fill_columns(columns, jnp.concatenate(
        [edges_ref[receiver:receiver + 1, step * 2048:step * 2048 + 2048] for step in range(4)], axis=0))

    def body(step, carry):
        part = span(step, 2048)
        found = read_table(table_ref, blocks, edges_ref[sender:sender + 1, part], 32)
        sums_ref[:used] += spread(found, blocks, edges_ref[receiver:receiver + 1, part], columns[step])
        return carry
    lax.fori_loop(0, 4, body, 0)
    return gathered_sums(sums_ref, blocks, 32)


def bias_columns(biases):
    rows = biases[...]
    return jnp.concatenate([rows, rows], axis=0).T


def extended(features, halo):
    return jnp.concatenate([features] + [halo[slot] for slot in range(4)], axis=1)


def put_slabs(out, values):
    for position in range(16):
        out[position] = values[:, position * 128:position * 128 + 128]


def gate(values):
    return 1.0 / (1.0 + jnp.exp(-values))


def silu_and_slope(values):
    opened = gate(values)
    silu = values * opened
    return silu, opened + silu * (1.0 - opened)


def fine_forward_kernel(scale, features, halo, sources, to_coarse, edge_in, edge_out, node_in, node_out, biases,
                        middle, slope, hidden, node_pre, pooled, table, received, columns, packed, *scratch):
    summing = WholeSum(16, packed, scratch)
    barrier = pltpu.get_barrier_semaphore()
    count = summing.greet(barrier)
    bias = bias_columns(biases)
    feats = features[...]
    weights = edge_in[...]
    received[...] = product(weights[:, :64], feats) + bias[:, 0:1]
    fill_table(table, product(weights[:, 64:], extended(feats, halo)))

    def body(step, carry):
        part = span(step, WIDTH)
        base = received[:, part]

        def edge(k, total):
            silu, slopes = silu_and_slope(base + read_table(table, EXT // RADIX, sources[pl.ds(k, 1), part]))
            slope[k, :, part] = slopes
            return total + silu
        hidden[:, part] = lax.fori_loop(0, 8, edge, jnp.zeros((64, WIDTH), jnp.float32))
        return carry
    lax.fori_loop(0, 2048 // WIDTH, body, 0)
    aggregate = product(edge_out[...], hidden[...])
    pre = product(node_in[...], jnp.concatenate([feats, aggregate], axis=0)) + bias[:, 1:2]
    node_pre[...] = pre
    middle[...] = feats + product(node_out[...], pre * gate(pre))
    put_slabs(packed, spread_all(columns, middle[...], to_coarse[...]) * scale)
    pl.semaphore_wait(barrier, count)
    summing.run()
    for position in range(16):
        pooled[:, position * 128:position * 128 + 128] = summing.slab(position)


def coarse_kernel(factor, pooled, coarse_in, coarse_out, coarse_mix, biases, edges, to_fine, middle, cotangent,
                  up_in, up_out, output, grad_middle, grad_mixed, mixed_back, mixed_sum, up_grads, table, looked,
                  sums, columns, packed, mine, theirs, mine_back, theirs_back, swap_sems, *scratch):
    summing = WholeSum(16, packed, scratch)
    barrier = pltpu.get_barrier_semaphore()
    count = summing.greet(barrier)
    bias = bias_columns(biases)
    first = jnp.broadcast_to(summing.core == 0, (32, 2048))
    values = pooled[...]
    pre = product(coarse_in[...], values) + bias[:, 2:3]
    nodes = values + product(coarse_out[...], pre * gate(pre))
    mine[...] = mix_half(sums, table, columns, edges, 0, 1, jnp.where(first, nodes[:32], nodes[32:]))
    pl.semaphore_wait(barrier, count)
    swap = copy_to(mine, theirs, swap_sems.at[0], swap_sems.at[1], summing.sibling)
    swap.start()
    swap.wait()
    summed = jnp.concatenate([jnp.where(first, mine[...], theirs[...]), jnp.where(first, theirs[...], mine[...])],
                             axis=0)
    mixed_sum[...] = summed
    fill_table(table, nodes + product(coarse_mix[...], summed) * factor)
    read_all(looked, table, to_fine, WIDTH)
    both = jnp.concatenate([middle[...], looked[...]], axis=0)
    silu, slopes = silu_and_slope(product(up_in[...], both) + bias[:, 3:4])
    output[...] = middle[...] + product(up_out[...], silu)
    cot = cotangent[...]
    grad_pre = product_tn(up_out[...], cot) * slopes
    up_grads[0] = product_nt(grad_pre, both)
    up_grads[1] = jnp.concatenate(
        [product_nt(cot, silu), jnp.broadcast_to(jnp.sum(grad_pre, axis=1, keepdims=True), (64, 64))], axis=1)
    grad_both = product_tn(up_in[...], grad_pre)
    grad_middle[...] = cot + grad_both[:64]
    put_slabs(packed, spread_all(columns, grad_both[64:], to_fine[...]))
    summing.run(back=False)
    summing.back_core().start()
    own_half = jnp.concatenate([summing.half_out[position] for position in range(16)], axis=1)
    mine_back[...] = mix_half(sums, table, columns, edges, 1, 0, own_half)
    swap = copy_to(mine_back, theirs_back, swap_sems.at[2], swap_sems.at[3], summing.sibling)
    swap.start()
    summing.back_core().wait()
    for position in range(16):
        grad_mixed[:, position * 128:position * 128 + 128] = summing.slab(position)
    swap.wait()
    mixed_back[:32] = jnp.where(first, mine_back[...], theirs_back[...])
    mixed_back[32:] = jnp.where(first, theirs_back[...], mine_back[...])


def backward_kernel(factor, scale, grad_mixed, mixed_back, mixed_sum, pooled, coarse_in, coarse_out, coarse_mix,
                    biases, to_coarse, grad_middle, node_pre, hidden, slope, features, halo, sources, edge_in,
                    edge_out, node_in, node_out, up_grads, rows, grad_features, weight_sums, coarse_grads, table,
                    found, scratch, sums, columns, own, grad_halo, packed, arrived_ref, sent, arrived, *sum_refs):
    summing = WholeSum(8, packed, sum_refs)
    barrier = pltpu.get_barrier_semaphore()
    count = summing.greet(barrier)
    greet_sides(barrier)
    bias = bias_columns(biases)
    packed[4:6] = up_grads[...]
    packed[6:8] = jnp.zeros((2, 64, 128), jnp.float32)
    grad_mix_all = grad_mixed[...]
    coarse_grads[:, 256:384] = jnp.concatenate(
        [product_nt(grad_mix_all, mixed_sum[...]) * factor, jnp.zeros((64, 64), jnp.float32)], axis=1)
    grad_nodes = grad_mix_all + product_tn(coarse_mix[...], mixed_back[...]) * factor
    values = pooled[...]
    silu, slopes = silu_and_slope(product(coarse_in[...], values) + bias[:, 2:3])
    grad_pre = product_tn(coarse_out[...], grad_nodes) * slopes
    coarse_grads[:, 0:128] = jnp.concatenate([product_nt(grad_pre, values), product_nt(grad_nodes, silu)], axis=1)
    coarse_grads[:, 128:256] = jnp.broadcast_to(jnp.sum(grad_pre, axis=1, keepdims=True), (64, 128))
    fill_table(table, grad_nodes + product_tn(coarse_in[...], grad_pre))
    read_all(found, table, to_coarse, WIDTH)
    grad_mid = grad_middle[...] + found[...] * scale
    feats = features[...]
    silu, slopes = silu_and_slope(node_pre[...])
    aggregate = product(edge_out[...], hidden[...])
    grad_pre = product_tn(node_out[...], grad_mid) * slopes
    packed[0] = product_nt(grad_pre, jnp.concatenate([feats, aggregate], axis=0))
    node_bias = jnp.sum(grad_pre, axis=1, keepdims=True)
    grad_both = product_tn(node_in[...], grad_pre)
    grad_sum = grad_both[64:]
    packed[1] = jnp.concatenate(
        [product_nt(grad_mid, silu), product_nt(grad_sum, hidden[...])], axis=1)
    found[...] = grad_mid + grad_both[:64]
    scratch[...] = product_tn(edge_out[...], grad_sum)
    blocks = EXT // RADIX
    sums[...] = jnp.zeros(sums.shape, jnp.float32)
    fill_columns(columns, sources[...])

    def body(step, carry):
        part = span(step, WIDTH)
        base = scratch[:, part]

        def edge(k, total):
            grad_edge = base * slope[k, :, part]
            sums[...] += spread(grad_edge, blocks, sources[pl.ds(k, 1), part], columns[k, part])
            return total + grad_edge
        scratch[:, part] = lax.fori_loop(0, 8, edge, jnp.zeros((64, WIDTH), jnp.float32))
        return carry
    lax.fori_loop(0, 2048 // WIDTH, body, 0)
    grad_sent = gathered_sums(sums, blocks)
    grad_received = scratch[...]
    packed[2] = jnp.concatenate(
        [product_nt(grad_received, feats),
         product_nt(grad_sent, extended(feats, halo))], axis=1)
    packed[3] = jnp.concatenate(
        [jnp.broadcast_to(jnp.sum(grad_received, axis=1, keepdims=True), (64, 64)),
         jnp.broadcast_to(node_bias, (64, 64))], axis=1)
    weights = edge_in[...]
    back = product_tn(weights[:, 64:], grad_sent)
    own[...] = found[...] + product_tn(weights[:, :64], grad_received) + back[:, :2048]
    for slot in range(4):
        grad_halo[slot] = back[:, 2048 + slot * 128:2048 + slot * 128 + 128]
    pl.semaphore_wait(barrier, count + 4)
    for slot in range(4):
        side_copy(grad_halo, arrived_ref, sent, arrived, slot, True).start()

    def add_returned():
        columns, parts = [], []
        for slot in range(4):
            side_copy(grad_halo, arrived_ref, sent, arrived, slot, True).wait()
            there = jnp.broadcast_to(side_exists(True)[slot], (64, 128))
            parts.append(jnp.where(there, arrived_ref[slot], 0.0))
        indices = rows[...]
        lows = (jnp.concatenate([indices, indices], axis=0) & (RADIX - 1)).astype(jnp.float32).T
        index_row = jnp.concatenate([indices[slot:slot + 1, :] for slot in range(4)], axis=1)
        low_column = jnp.concatenate([lows[:, slot:slot + 1] for slot in range(4)], axis=0)
        blocks = COARSE // RADIX
        found = spread(jnp.concatenate(parts, axis=1), blocks, index_row, low_column)
        for block in range(blocks):
            part = slice(block * RADIX, (block + 1) * RADIX)
            grad_features[:, part] = own[:, part] + found[block * 64:block * 64 + 64]
    summing.run(add_returned)
    for position in range(8):
        weight_sums[position] = summing.slab(position)


def call(kernel, outs, scratch, *operands):
    return pl.pallas_call(
        kernel,
        out_shape=[jax.ShapeDtypeStruct(shape, jnp.float32) for shape in outs],
        in_specs=[pl.BlockSpec(memory_space=pltpu.VMEM)] * len(operands),
        out_specs=[pl.BlockSpec(memory_space=pltpu.VMEM)] * len(outs),
        scratch_shapes=[pltpu.VMEM(shape, dtype) for shape, dtype in scratch],
        compiler_params=pltpu.CompilerParams(vmem_limit_bytes=VMEM_LIMIT),
    )(*operands)


def copy_to(source, target, sent, arrived, device):
    return pltpu.make_async_remote_copy(
        src_ref=source, dst_ref=target, send_sem=sent, recv_sem=arrived, device_id=device, device_id_type=MESH)


def each(make, count):
    for k in range(1, count):
        make(k).start()
    for k in range(1, count):
        make(k).wait()


def turned(place, count):
    return jnp.where(place >= count, place - count, place)


def side_devices(back):
    gx, gy = lax.axis_index("gx"), lax.axis_index("gy")
    up, down = (lax.rem(gx + 1, 8), gy), (lax.rem(gx + 7, 8), gy)
    right, left = (gx, lax.rem(gy + 1, 32)), (gx, lax.rem(gy + 31, 32))
    return (down, up, left, right) if back else (up, down, right, left)


def side_exists(back):
    gx, gy = lax.axis_index("gx"), lax.axis_index("gy")
    below = (gx > 0, gx < 7, gy > 0, gy < 31)
    return (below[1], below[0], below[3], below[2]) if back else below


def greet_sides(barrier):
    for device in side_devices(False):
        pl.semaphore_signal(barrier, inc=1, device_id=device, device_id_type=MESH)


class WholeSum:
    def __init__(self, slabs, x_ref, scratch):
        (self.half, self.core_parts, self.flat_parts, self.piece, self.line_parts, self.half_out, self.other,
         self.core_sems, self.flat_sent, self.flat_arrived, self.line_sent, self.line_arrived,
         self.back_sent, self.back_arrived) = scratch
        self.slabs, self.rows, self.x_ref = slabs, 2 * slabs, x_ref
        gx, gy = lax.axis_index("gx"), lax.axis_index("gy")
        self.x, self.y = gx // 2, gy // 8
        self.core, self.z = gx - 2 * self.x, gy - 8 * self.y
        self.gx, self.gy = gx, gy
        self.sibling = (gx + 1 - 2 * self.core, gy)
        self.xs = [turned(self.x + k, 4) for k in range(4)]
        self.ys = [turned(self.y + k, 4) for k in range(4)]
        self.zs = [turned(self.z + k, 8) for k in range(8)]

    def flat_device(self, k):
        return (self.xs[k // 4] * 2 + self.core, self.ys[k % 4] * 8 + self.z)

    def line_device(self, k):
        return (self.gx, self.y * 8 + self.zs[k])

    def chunk(self, ref, k):
        x, y = self.xs[k // 4], self.ys[k % 4]
        if self.rows == 32:
            return ref.at[x * 4 + y]
        high = y // 2
        return ref.at[x * 2 + high, pl.ds(pl.multiple_of((y - 2 * high) * 16, 16), 16)]

    def own_rows(self, core):
        return pl.ds(pl.multiple_of(core * 32, 32), 32)

    def greet(self, barrier):
        devices = ([self.sibling] + [self.line_device(k) for k in range(1, 8)]
                   + [self.flat_device(k) for k in range(1, 16)])
        for device in devices:
            pl.semaphore_signal(barrier, inc=1, device_id=device, device_id_type=MESH)
        return len(devices)

    def to_core(self):
        return copy_to(self.x_ref.at[:, self.own_rows(1 - self.core)], self.core_parts,
                       self.core_sems.at[0], self.core_sems.at[1], self.sibling)

    def to_flat(self, k):
        return copy_to(self.chunk(self.half, k), self.flat_parts.at[k], self.flat_sent.at[k],
                       self.flat_arrived.at[k], self.flat_device(k))

    def to_line(self, k):
        return copy_to(self.piece, self.line_parts.at[self.z], self.line_sent.at[k], self.line_arrived.at[k],
                       self.line_device(k))

    def back_flat(self, k):
        mine = self.chunk(self.half_out, 0)
        return copy_to(mine, mine, self.back_sent.at[k], self.back_arrived.at[k], self.flat_device(k))

    def back_core(self):
        return copy_to(self.half_out, self.other, self.core_sems.at[2], self.core_sems.at[3], self.sibling)

    def run(self, beside=None, back=True):
        self.to_core().start()
        if beside is not None:
            beside()
        self.to_core().wait()
        self.half[...] = self.x_ref[:, self.own_rows(self.core)] + self.core_parts[...]
        each(self.to_flat, 16)
        total = self.chunk(self.half, 0)[...]
        for k in range(1, 16):
            total = total + self.flat_parts[k]
        self.piece[...] = total
        self.line_parts[self.z] = total
        each(self.to_line, 8)
        total = self.line_parts[0]
        for k in range(1, 8):
            total = total + self.line_parts[k]
        self.chunk(self.half_out, 0)[...] = total
        each(self.back_flat, 16)
        if back:
            self.back_core().start()
            self.back_core().wait()

    def slab(self, position):
        first = jnp.broadcast_to(self.core == 0, (32, 128))
        own, other = self.half_out[position], self.other[position]
        return jnp.concatenate([jnp.where(first, own, other), jnp.where(first, other, own)], axis=0)


def sum_scratch(slabs):
    rows, dma = 2 * slabs, pltpu.SemaphoreType.DMA
    half = pltpu.VMEM((slabs, 32, 128), jnp.float32)
    return [half, half, pltpu.VMEM((16, rows, 128), jnp.float32), pltpu.VMEM((rows, 128), jnp.float32),
            pltpu.VMEM((8, rows, 128), jnp.float32), half, half,
            dma((4,)), dma((16,)), dma((16,)), dma((8,)), dma((8,)), dma((16,)), dma((16,))]


def remote_call(kernel, outs, scratch, collective_id, *operands):
    return pl.pallas_call(
        kernel,
        out_shape=[jax.ShapeDtypeStruct(shape, jnp.float32) for shape in outs],
        in_specs=[pl.BlockSpec(memory_space=pltpu.VMEM)] * len(operands),
        out_specs=[pl.BlockSpec(memory_space=pltpu.VMEM)] * len(outs),
        scratch_shapes=scratch,
        compiler_params=pltpu.CompilerParams(collective_id=collective_id, has_side_effects=True,
                                             vmem_limit_bytes=VMEM_LIMIT),
    )(*operands)


def side_copy(packets, arrived_ref, sent, arrived, slot, back):
    return copy_to(packets.at[slot], arrived_ref.at[slot], sent.at[slot], arrived.at[slot], side_devices(back)[slot])


def halo_kernel(features, rows, halo, table, packets, arrived_ref, sent, arrived):
    barrier = pltpu.get_barrier_semaphore()
    greet_sides(barrier)
    fill_table(table, features[...])
    for slot in range(4):
        packets[slot] = read_table(table, COARSE // RADIX, rows[slot:slot + 1, :])
    pl.semaphore_wait(barrier, 4)
    for slot in range(4):
        side_copy(packets, arrived_ref, sent, arrived, slot, False).start()
    for slot in range(4):
        side_copy(packets, arrived_ref, sent, arrived, slot, False).wait()
        there = jnp.broadcast_to(side_exists(False)[slot], (64, 128))
        halo[slot] = jnp.where(there, arrived_ref[slot], 0.0)


def exchange(features, rows):
    dma = pltpu.SemaphoreType.DMA
    slots = pltpu.VMEM((4, 64, 128), jnp.float32)
    halo, = remote_call(
        halo_kernel, [(4, 64, 128)],
        [pltpu.VMEM((COARSE // RADIX * 64, 2 * RADIX), jnp.bfloat16), slots, slots, dma((4,)), dma((4,))],
        1, features, rows)
    return halo


def unpack_kernel(output, grad_features, weight_sums, coarse_grads, out, out_features, grad_edge_in, grad_edge_out,
                  grad_node_in, grad_node_out, grad_coarse_in, grad_coarse_out, grad_coarse_mix, grad_up_in,
                  grad_up_out, grad_biases):
    out[...] = output[...]
    out_features[...] = grad_features[...]
    grad_node_in[...] = weight_sums[0]
    pair = weight_sums[1]
    grad_node_out[...] = pair[:, :64]
    grad_edge_out[...] = pair[:, 64:]
    grad_edge_in[...] = weight_sums[2]
    grad_up_in[...] = weight_sums[4]
    last = weight_sums[5]
    grad_up_out[...] = last[:, :64]
    grad_coarse_in[...] = coarse_grads[:, 0:64]
    grad_coarse_out[...] = coarse_grads[:, 64:128]
    grad_coarse_mix[...] = coarse_grads[:, 256:320]
    fine_bias, up_bias, coarse_bias = weight_sums[3].T, last.T, coarse_grads[:, 128:256].T
    grad_biases[...] = jnp.concatenate(
        [fine_bias[0:1], fine_bias[64:65], coarse_bias[0:1], up_bias[64:65]], axis=0)


def local(
    features,
    cotangent,
    edge_src,
    send_rows,
    fine_to_coarse,
    coarse_to_fine,
    coarse_edges,
    edge_in,
    edge_out,
    node_in,
    node_out,
    coarse_in,
    coarse_out,
    coarse_mix,
    up_in,
    up_out,
    biases,
):
    scale = (COARSE / (features.shape[1] * lax.axis_size("gx") * lax.axis_size("gy"))) ** 0.5
    factor = (COARSE / coarse_edges.shape[1]) ** 0.5
    f32, dma = jnp.float32, pltpu.SemaphoreType.DMA
    to_coarse, to_fine = fine_to_coarse.reshape(1, -1), coarse_to_fine.reshape(1, -1)
    table = pltpu.VMEM((EXT // RADIX * 64, 2 * RADIX), jnp.bfloat16)
    sums, columns = pltpu.VMEM((EXT // RADIX * 64, RADIX), f32), pltpu.VMEM((8, 2048, 1), f32)
    wide, half = pltpu.VMEM((64, 2048), f32), pltpu.VMEM((32, 2048), f32)
    slots = pltpu.VMEM((4, 64, 128), f32)
    halo = exchange(features, send_rows)
    middle, slope, hidden, node_pre, pooled = remote_call(
        partial(fine_forward_kernel, scale),
        [(64, 2048), (8, 64, 2048), (64, 2048), (64, 2048), (64, 2048)],
        [table, wide, columns, pltpu.VMEM((16, 64, 128), f32), *sum_scratch(16)], 2,
        features, halo, edge_src, to_coarse, edge_in, edge_out, node_in, node_out, biases)
    output, grad_middle, grad_mixed, mixed_back, mixed_sum, up_grads = remote_call(
        partial(coarse_kernel, factor),
        [(64, 2048), (64, 2048), (64, 2048), (64, 2048), (64, 2048), (2, 64, 128)],
        [table, wide, sums, columns, pltpu.VMEM((16, 64, 128), f32), half, half, half, half, dma((4,)),
         *sum_scratch(16)], 3,
        pooled, coarse_in, coarse_out, coarse_mix, biases, coarse_edges, to_fine, middle, cotangent, up_in, up_out)
    grad_features, weight_sums, coarse_grads = remote_call(
        partial(backward_kernel, factor, scale),
        [(64, 2048), (8, 64, 128), (64, 384)],
        [table, wide, wide, sums, columns, wide, slots, pltpu.VMEM((8, 64, 128), f32), slots, dma((4,)), dma((4,)),
         *sum_scratch(8)], 4,
        grad_mixed, mixed_back, mixed_sum, pooled, coarse_in, coarse_out, coarse_mix, biases, to_coarse,
        grad_middle, node_pre, hidden, slope, features, halo, edge_src, edge_in, edge_out, node_in, node_out,
        up_grads, send_rows)
    (out, out_features, grad_edge_in, grad_edge_out, grad_node_in, grad_node_out, grad_coarse_in, grad_coarse_out,
     grad_coarse_mix, grad_up_in, grad_up_out, grad_biases) = call(
        unpack_kernel,
        [(64, 2048), (64, 2048), (64, 128), (64, 64), (64, 128), (64, 64), (64, 64), (64, 64), (64, 64), (64, 128),
         (64, 64), (4, 64)], [], output, grad_features, weight_sums, coarse_grads)
    return (out, out_features, grad_edge_in, grad_edge_out, grad_node_in, grad_node_out, grad_coarse_in,
            grad_coarse_out, grad_coarse_mix, grad_up_in, grad_up_out, grad_biases)


def solution(mesh):
    in_specs = (
        P(None, ("gx", "gy")),
        P(None, ("gx", "gy")),
        P(None, ("gx", "gy")),
        P(None, ("gx", "gy")),
        P(("gx", "gy")),
        P(("gx", "gy")),
        P(),
        P(),
        P(),
        P(),
        P(),
        P(),
        P(),
        P(),
        P(),
        P(),
        P(),
    )
    out_specs = (
        P(None, ("gx", "gy")),
        P(None, ("gx", "gy")),
        P(),
        P(),
        P(),
        P(),
        P(),
        P(),
        P(),
        P(),
        P(),
        P(),
    )
    return jax.shard_map(local, mesh=mesh, in_specs=in_specs, out_specs=out_specs, check_vma=False)
```

time: 193 us -> 156 us (0.81)
  Pallas kernels: 177 us -> 155 us
  local copies, waits for them, and re-layouts: 14.3 us -> 0 us
    pallas_call x3 -> x1, Pallas kernels: 80.4 us -> 2.4 us  [call(): pl.pallas_call(kernel, out_shape=[jax.ShapeDtypeStruct(shape, jnp.float32...]
    pallas_call x4, Pallas kernels: 96.3 us -> 152 us  [remote_call(): pl.pallas_call(kernel, out_shape=[jax.ShapeDtypeStruct(shape, jnp.float32...]
    unnamed x9 -> x0, local copies, waits for them, and re-layouts: 12.8 us -> none
where the time goes in v3:
time: 156 us; the launch traced here: 155 us
  Pallas kernels  155 us (99%)
    pallas_call x4, Pallas kernels, remote_call(): pl.pallas_call(kernel, out_shape=[jax.ShapeDtypeStruct(shape, jnp.float32...  152 us

profile of v3, /device:TPU:1, one launch (start us, length us, event | category | flops | bytes accessed | tf_op | source)
XLA Modules:
  0.0 155.4 jit_solution(16365498808834481660)
XLA Ops:
  0.6 14.7 %shard_map.256.halo = f32[4,64,128]{2,1,0:T(8,128)} custom-call(f32[64,2048]{1,0:T(8,128)} %features.5, s32[4,128]{1,0:T(4,128)} %rows.3), custom_call_target="tpu_custom_call" | custom-call | tf_op jit(solution)/shard_map/pallas_call | solution.py:464
  15.4 41.7 %shard_map.257 = (f32[64,2048]{1,0:T(8,128)}, f32[8,64,2048]{2,1,0:T(8,128)}, f32[64,2048]{1,0:T(8,128)}, f32[64,2048]{1,0:T(8,128)}, f32[64,2048]{1,0:T(8,128)}) custom-call(f32[64,2048]{1,0:T(8,128)} %features.5, f32[4,64,128]{2,1,0:T(8,128)} %shard_map.256.halo, s32[8,2048]{1,0:T(8,128)} %sources.3, s32[1,2048]{1,0:T(1,128)} %bitcast.2, ...), custom_call_target="tpu_custom_call" | custom-call | tf_op jit(solution)/shard_map/pallas_call | solution.py:464
  57.1 51.8 %shard_map.258 = (f32[64,2048]{1,0:T(8,128)}, f32[64,2048]{1,0:T(8,128)}, f32[64,2048]{1,0:T(8,128)}, f32[64,2048]{1,0:T(8,128)}, f32[64,2048]{1,0:T(8,128)}, /*index=5*/f32[2,64,128]{2,1,0:T(8,128)}) custom-call(f32[64,2048]{1,0:T(8,128)} %get-tuple-element.26.pooled, f32[64,64]{1,0:T(8,128)} %coarse_in.3, f32[64,64]{1,0:T(8,128)} %coarse_out.3, ...), custom_call_target="tpu_custom_call" | custom-call | tf_op jit(solution)/shard_map/pallas_call | solution.py:464
  108.9 44.0 %shard_map.259 = (f32[64,2048]{1,0:T(8,128)}, f32[8,64,128]{2,1,0:T(8,128)}, f32[64,384]{1,0:T(8,128)}) custom-call(f32[64,2048]{1,0:T(8,128)} %get-tuple-element.29.grad_mixed, f32[64,2048]{1,0:T(8,128)} %get-tuple-element.30.mixed_back, f32[64,2048]{1,0:T(8,128)} %get-tuple-element.31.mixed_sum, f32[64,2048]{1,0:T(8,128)} %get-tuple-element.26.pooled, ...), custom_call_target="tpu_custom_call" | custom-call | tf_op jit(solution)/shard_map/pallas_call | solution.py:464
  152.9 2.4 %shard_map.260 = (f32[64,2048]{1,0:T(8,128)}, f32[64,2048]{1,0:T(8,128)}, f32[64,128]{1,0:T(8,128)}, f32[64,64]{1,0:T(8,128)}, f32[64,128]{1,0:T(8,128)}, /*inde...) custom-call(f32[64,2048]{1,0:T(8,128)} %get-tuple-element.28.output,, ...), custom_call_target="tpu_custom_call" | custom-call | tf_op jit(solution)/shard_map/pallas_call | solution.py:326

commit v4 on v3

--- a/solution.py
+++ b/solution.py
@@ -67,6 +67,20 @@
     for block in range(1, blocks):
         total = jnp.where(chosen == block, found[block * height:(block + 1) * height], total)
     return total
+
+
+def lane_gather(table_ref, first, index_row, start):
+    pieces = []
+    for piece in range(index_row.shape[1] // 128):
+        row = index_row[:, piece * 128:piece * 128 + 128]
+        lanes = jnp.broadcast_to(row & 127, (64, 128))
+        chosen = jnp.broadcast_to(row >> 7, (64, 128))
+        total = start[:, piece * 128:piece * 128 + 128]
+        for block in range(table_ref.shape[1] // 128):
+            found = jnp.take_along_axis(table_ref[:, block * 128:block * 128 + 128], lanes, axis=1)
+            total = jnp.where(chosen == first + block, found, total)
+        pieces.append(total)
+    return jnp.concatenate(pieces, axis=1)
 
 
 def spread(values, blocks, index_row, low_column):
@@ -128,7 +142,7 @@
         found = read_table(table_ref, blocks, edges_ref[sender:sender + 1, part], 32)
         sums_ref[:used] += spread(found, blocks, edges_ref[receiver:receiver + 1, part], columns[step])
         return carry
-    lax.fori_loop(0, 4, body, 0)
+    lax.fori_loop(0, 4, body, 0, unroll=4)
     return gathered_sums(sums_ref, blocks, 32)
 
 
@@ -157,7 +171,7 @@
 
 
 def fine_forward_kernel(scale, features, halo, sources, to_coarse, edge_in, edge_out, node_in, node_out, biases,
-                        middle, slope, hidden, node_pre, pooled, table, received, columns, packed, *scratch):
+                        middle, slope, hidden, node_pre, pooled, table, received, columns, packed, tail, *scratch):
     summing = WholeSum(16, packed, scratch)
     barrier = pltpu.get_barrier_semaphore()
     count = summing.greet(barrier)
@@ -165,17 +179,21 @@
     feats = features[...]
     weights = edge_in[...]
     received[...] = product(weights[:, :64], feats) + bias[:, 0:1]
-    fill_table(table, product(weights[:, 64:], extended(feats, halo)))
+    sender_part = product(weights[:, 64:], extended(feats, halo))
+    fill_table(table, sender_part[:, :COARSE])
+    tail[...] = sender_part[:, COARSE:]
 
     def body(step, carry):
         part = span(step, WIDTH)
         base = received[:, part]
 
         def edge(k, total):
-            silu, slopes = silu_and_slope(base + read_table(table, EXT // RADIX, sources[pl.ds(k, 1), part]))
+            row = sources[pl.ds(k, 1), part]
+            found = lane_gather(tail, COARSE // 128, row, read_table(table, COARSE // RADIX, row))
+            silu, slopes = silu_and_slope(base + found)
             slope[k, :, part] = slopes
             return total + silu
-        hidden[:, part] = lax.fori_loop(0, 8, edge, jnp.zeros((64, WIDTH), jnp.float32))
+        hidden[:, part] = lax.fori_loop(0, 8, edge, jnp.zeros((64, WIDTH), jnp.float32), unroll=4)
         return carry
     lax.fori_loop(0, 2048 // WIDTH, body, 0)
     aggregate = product(edge_out[...], hidden[...])
@@ -282,7 +300,7 @@
             grad_edge = base * slope[k, :, part]
             sums[...] += spread(grad_edge, blocks, sources[pl.ds(k, 1), part], columns[k, part])
             return total + grad_edge
-        scratch[:, part] = lax.fori_loop(0, 8, edge, jnp.zeros((64, WIDTH), jnp.float32))
+        scratch[:, part] = lax.fori_loop(0, 8, edge, jnp.zeros((64, WIDTH), jnp.float32), unroll=4)
         return carry
     lax.fori_loop(0, 2048 // WIDTH, body, 0)
     grad_sent = gathered_sums(sums, blocks)
@@ -553,7 +571,7 @@
     middle, slope, hidden, node_pre, pooled = remote_call(
         partial(fine_forward_kernel, scale),
         [(64, 2048), (8, 64, 2048), (64, 2048), (64, 2048), (64, 2048)],
-        [table, wide, columns, pltpu.VMEM((16, 64, 128), f32), *sum_scratch(16)], 2,
+        [table, wide, columns, pltpu.VMEM((16, 64, 128), f32), pltpu.VMEM((64, 512), f32), *sum_scratch(16)], 2,
         features, halo, edge_src, to_coarse, edge_in, edge_out, node_in, node_out, biases)
     output, grad_middle, grad_mixed, mixed_back, mixed_sum, up_grads = remote_call(
         partial(coarse_kernel, factor),

time: 156 us -> 145 us (0.929)
  Pallas kernels: 155 us -> 144 us
    pallas_call x4, Pallas kernels: 152 us -> 142 us  [remote_call(): pl.pallas_call(kernel, out_shape=[jax.ShapeDtypeStruct(shape, jnp.float32...]
where the time goes in v4:
time: 145 us
  Pallas kernels  144 us (99%)
    pallas_call x4, Pallas kernels, remote_call(): pl.pallas_call(kernel, out_shape=[jax.ShapeDtypeStruct(shape, jnp.float32...  142 us

profile of v4, /device:TPU:1, one launch (start us, length us, event | category | flops | bytes accessed | tf_op | source)
XLA Modules:
  0.0 145.1 jit_solution(18334569762147140540)
XLA Ops:
  0.6 14.7 %shard_map.256.halo = f32[4,64,128]{2,1,0:T(8,128)} custom-call(f32[64,2048]{1,0:T(8,128)} %features.5, s32[4,128]{1,0:T(4,128)} %rows.3), custom_call_target="tpu_custom_call" | custom-call | tf_op jit(solution)/shard_map/pallas_call | solution.py:482
  15.4 38.2 %shard_map.257 = (f32[64,2048]{1,0:T(8,128)}, f32[8,64,2048]{2,1,0:T(8,128)}, f32[64,2048]{1,0:T(8,128)}, f32[64,2048]{1,0:T(8,128)}, f32[64,2048]{1,0:T(8,128)}) custom-call(f32[64,2048]{1,0:T(8,128)} %features.5, f32[4,64,128]{2,1,0:T(8,128)} %shard_map.256.halo, s32[8,2048]{1,0:T(8,128)} %sources.3, s32[1,2048]{1,0:T(1,128)} %bitcast.2, ...), custom_call_target="tpu_custom_call" | custom-call | tf_op jit(solution)/shard_map/pallas_call | solution.py:482
  53.6 46.2 %shard_map.258 = (f32[64,2048]{1,0:T(8,128)}, f32[64,2048]{1,0:T(8,128)}, f32[64,2048]{1,0:T(8,128)}, f32[64,2048]{1,0:T(8,128)}, f32[64,2048]{1,0:T(8,128)}, /*index=5*/f32[2,64,128]{2,1,0:T(8,128)}) custom-call(f32[64,2048]{1,0:T(8,128)} %get-tuple-element.26.pooled, f32[64,64]{1,0:T(8,128)} %coarse_in.3, f32[64,64]{1,0:T(8,128)} %coarse_out.3, ...), custom_call_target="tpu_custom_call" | custom-call | tf_op jit(solution)/shard_map/pallas_call | solution.py:482
  99.8 42.8 %shard_map.259 = (f32[64,2048]{1,0:T(8,128)}, f32[8,64,128]{2,1,0:T(8,128)}, f32[64,384]{1,0:T(8,128)}) custom-call(f32[64,2048]{1,0:T(8,128)} %get-tuple-element.29.grad_mixed, f32[64,2048]{1,0:T(8,128)} %get-tuple-element.30.mixed_back, f32[64,2048]{1,0:T(8,128)} %get-tuple-element.31.mixed_sum, f32[64,2048]{1,0:T(8,128)} %get-tuple-element.26.pooled, ...), custom_call_target="tpu_custom_call" | custom-call | tf_op jit(solution)/shard_map/pallas_call | solution.py:482
  142.5 2.4 %shard_map.260 = (f32[64,2048]{1,0:T(8,128)}, f32[64,2048]{1,0:T(8,128)}, f32[64,128]{1,0:T(8,128)}, f32[64,64]{1,0:T(8,128)}, f32[64,128]{1,0:T(8,128)}, /*inde...) custom-call(f32[64,2048]{1,0:T(8,128)} %get-tuple-element.28.output,, ...), custom_call_target="tpu_custom_call" | custom-call | tf_op jit(solution)/shard_map/pallas_call | solution.py:344

commit v5 on v4

--- a/solution.py
+++ b/solution.py
@@ -12,7 +12,7 @@
 RADIX = 256
 SHIFT = 8
 WIDTH = 2048
-VMEM_LIMIT = 56 * 2**20
+VMEM_LIMIT = 44 * 2**20
 
 
 MESH = pl.DeviceIdType.MESH

time: 145 us -> 153 us (1.055); the launches traced: 145 us -> 151 us
  local copies, waits for them, and re-layouts: 0 us -> 21 us
  Pallas kernels: 144 us -> 129 us
    unnamed x0 -> x54, local copies, waits for them, and re-layouts: none -> 21 us
    pallas_call x4, Pallas kernels: 142 us -> 128 us  [remote_call(): pl.pallas_call(kernel, out_shape=[jax.ShapeDtypeStruct(shape, jnp.float32...]
where the time goes in v5:
time: 153 us; the launch traced here: 151 us
  Pallas kernels  129 us (84%)
  local copies, waits for them, and re-layouts  21 us (14%)
    pallas_call x4, Pallas kernels, remote_call(): pl.pallas_call(kernel, out_shape=[jax.ShapeDtypeStruct(shape, jnp.float32...  128 us
    unnamed x54, local copies, waits for them, and re-layouts  21 us

profile of v5, /device:TPU:1, one launch (start us, length us, event | category | flops | bytes accessed | tf_op | source)
XLA Modules:
  0.0 151.1 jit_solution(16861601878333978813)
XLA Ops:
  0.6 0.0 copy-start
  0.7 1.0 copy-done
  1.7 0.0 copy-start.25
  1.7 0.7 copy-done.25
  2.4 12.9 %shard_map.256.halo = f32[4,64,128]{2,1,0:T(8,128)S(1)} custom-call(f32[64,2048]{1,0:T(8,128)S(1)} %copy-done, s32[4,128]{1,0:T(4,128)S(1)} %copy-done.25), custom_call_target="tpu_custom_call" | custom-call | tf_op jit(solution)/shard_map/pallas_call | solution.py:482
  15.3 0.0 copy-start.3
  15.3 0.8 copy-done.3
  16.1 0.0 copy-start.8
  16.1 0.8 copy-done.8
  16.9 0.0 copy-start.10
  16.9 0.8 copy-done.10
  17.6 0.0 copy-start.12
  17.6 0.8 copy-done.12
  18.4 0.0 copy-start.14
  18.4 0.8 copy-done.14
  19.1 0.0 copy-start.19
  19.1 0.7 copy-done.19
  19.8 0.0 copy-start.21
  19.8 0.7 copy-done.21
  20.5 34.2 %shard_map.257 = (f32[64,2048]{1,0:T(8,128)S(1)}, f32[8,64,2048]{2,1,0:T(8,128)S(1)}, f32[64,2048]{1,0:T(8,128)S(1)}, f32[64,2048]{1,0:T(8,128)S(1)}, f32[64,2048]{1,0:T(8,128)S(1)}) custom-call(f32[64,2048]{1,0:T(8,128)S(1)} %copy-done, f32[4,64,128]{2,1,0:T(8,128)S(1)} %shard_map.256.halo, s32[8,2048]{1,0:T(8,128)S(1)} %copy-done.3, ...), custom_call_target="tpu_custom_call" | custom-call | tf_op jit(solution)/shard_map/pallas_call | solution.py:482
  54.7 0.0 copy-start.2
  54.8 1.0 copy-done.2
  55.8 0.0 copy-start.5
  55.8 0.8 copy-done.5
  56.6 0.0 copy-start.6
  56.6 0.8 copy-done.6
  57.3 0.0 copy-start.7
  57.3 0.8 copy-done.7
  58.1 0.0 copy-start.16
  58.1 0.8 copy-done.16
  58.9 0.0 copy-start.17
  58.9 0.8 copy-done.17
  59.7 0.8 copy-done.18
  60.4 0.7 copy-done.22
  61.1 0.7 copy-done.24
  61.8 43.2 %shard_map.258 = (f32[64,2048]{1,0:T(8,128)S(1)}, f32[64,2048]{1,0:T(8,128)S(1)}, f32[64,2048]{1,0:T(8,128)S(1)}, f32[64,2048]{1,0:T(8,128)S(1)}, f32[64,2048]{1,0:T(8,128)S(1)}, /*index=5*/f32[2,64,128]{2,1,0:T(8,128)S(1)}) custom-call(f32[64,2048]{1,0:T(8,128)S(1)} %get-tuple-element.26.pooled, f32[64,64]{1,0:T(8,128)S(1)} %copy-done.5, ...), custom_call_target="tpu_custom_call" | custom-call | tf_op jit(solution)/shard_map/pallas_call | solution.py:482
  105.0 0.0 copy-start.1
  105.0 1.0 copy-done.1
  106.0 0.8 copy-done.4
  106.9 0.8 copy-done.9
  107.6 0.8 copy-done.11
  108.4 0.8 copy-done.13
  109.2 0.8 copy-done.15
  109.9 0.7 copy-done.20
  110.6 0.7 copy-done.23
  111.3 0.7 copy-done.26
  112.0 37.9 %shard_map.259 = (f32[64,2048]{1,0:T(8,128)S(1)}, f32[8,64,128]{2,1,0:T(8,128)S(1)}, f32[64,384]{1,0:T(8,128)S(1)}) custom-call(f32[64,2048]{1,0:T(8,128)S(1)} %get-tuple-element.29.grad_mixed, f32[64,2048]{1,0:T(8,128)S(1)} %get-tuple-element.30.mixed_back, f32[64,2048]{1,0:T(8,128)S(1)} %get-tuple-element.31.mixed_sum, ...), custom_call_target="tpu_custom_call" | custom-call | tf_op jit(solution)/shard_map/pallas_call | solution.py:482
  149.9 1.1 shard_map.260
  (11 shorter events, 0.0 us)
Async XLA Ops:
  0.6 1.0 copy-start
  1.7 0.7 copy-start.25
  15.3 0.8 copy-start.3
  16.1 0.8 copy-start.8
  16.9 0.8 copy-start.10
  17.6 0.8 copy-start.12
  18.4 0.8 copy-start.14
  19.1 0.7 copy-start.19
  19.8 0.7 copy-start.21
  54.7 1.0 copy-start.2
  55.8 0.8 copy-start.5
  56.6 0.8 copy-start.6
  57.3 0.8 copy-start.7
  58.1 0.8 copy-start.16
  58.9 0.8 copy-start.17
  59.7 0.8 copy-start.18
  60.4 0.7 copy-start.22
  61.1 0.7 copy-start.24
  105.0 1.0 copy-start.1
  106.0 0.8 copy-start.4
  106.9 0.8 copy-start.9
  107.6 0.8 copy-start.11
  108.4 0.8 copy-start.13
  109.2 0.8 copy-start.15
  109.9 0.7 copy-start.20
  110.6 0.7 copy-start.23
  111.3 0.7 copy-start.26
